TPU v7x, 32 devices: a whole 2x2x4 slice. The times are simulated.
32 devices in a mesh: seq: 8 (over y, x, core), fsdp: 4 (over z).
Axes of the slice: x: 2, y: 2, z: 4, core: 2. Of those that a mesh axis runs over, the one named last changes fastest.
Arguments:
- block_input: float32 [4, 1024, 1024], P('fsdp', 'seq'), may hold values from -6 to 6
- attn_gain: bfloat16 [1024], P('fsdp'), may hold values from 0.099609375 to 1.8984375
- query_weight: bfloat16 [1024, 512], P('fsdp'), may hold values from -0.1875 to 0.1875
- key_weight: bfloat16 [1024, 512], P('fsdp'), may hold values from -0.1875 to 0.1875
- value_weight: bfloat16 [1024, 1024], P('fsdp'), may hold values from -0.1875 to 0.1875
- gate_weight: bfloat16 [1024, 1024], P('fsdp'), may hold values from -0.1875 to 0.1875
- decay_down: bfloat16 [1024, 16], P('fsdp'), may hold values from -0.1875 to 0.1875
- decay_up: bfloat16 [16, 512], P(None, 'fsdp'), may hold values from -1.5 to 1.5
- decay_bias: bfloat16 [512], P('fsdp'), may hold values from -0.5 to 11
- head_gain: bfloat16 [256], P('fsdp'), may hold values from 0.099609375 to 1.8984375
- out_weight: bfloat16 [1024, 1024], P('fsdp'), may hold values from -0.375 to 0.375
- ffn_gain: bfloat16 [1024], P('fsdp'), may hold values from 0.099609375 to 1.8984375
- ffn_gate: bfloat16 [1024, 2816], P('fsdp'), may hold values from -0.1875 to 0.1875
- ffn_up: bfloat16 [1024, 2816], P('fsdp'), may hold values from -0.1875 to 0.1875
- ffn_down: bfloat16 [2816, 1024], P(None, 'fsdp'), may hold values from -0.21875 to 0.21875
- cotangent: float32 [4, 1024, 1024], P('fsdp', 'seq'), may hold values from -6 to 6
Outputs:
- block_output: float32 [4, 1024, 1024], P('fsdp', 'seq')
- input_grad: float32 [4, 1024, 1024], P('fsdp', 'seq')
- grad_attn_gain: float32 [1024], P(('seq', 'fsdp'))
- grad_query: float32 [1024, 512], P(('seq', 'fsdp'))
- grad_key: float32 [1024, 512], P(('seq', 'fsdp'))
- grad_value: float32 [1024, 1024], P(('seq', 'fsdp'))
- grad_gate: float32 [1024, 1024], P(('seq', 'fsdp'))
- grad_decay_down: float32 [1024, 16], P(('seq', 'fsdp'))
- grad_decay_up: float32 [16, 512], P(None, ('seq', 'fsdp'))
- grad_decay_bias: float32 [512], P(('seq', 'fsdp'))
- grad_head_gain: float32 [256], P(('seq', 'fsdp'))
- grad_out: float32 [1024, 1024], P(('seq', 'fsdp'))
- grad_ffn_gain: float32 [1024], P(('seq', 'fsdp'))
- grad_ffn_gate: float32 [1024, 2816], P(('seq', 'fsdp'))
- grad_ffn_up: float32 [1024, 2816], P(('seq', 'fsdp'))
- grad_ffn_down: float32 [2816, 1024], P(None, ('seq', 'fsdp'))
All inputs are finite; a program needn't handle non-finite values.
Results may differ from a plain program's by a relative error of at most 0.039.
Values may be sent and summed in bfloat16 or wider, within the bound.
A program may use at most 192 MiB of HBM per device.

v0:
```python
import jax
import jax.numpy as jnp
from jax import lax
from jax.sharding import PartitionSpec as P

H = 4
HK = 128
HV = 256
BLOCK = 64


norm_eps = 1e-06
logit_norm = 16.0
highest_precision = lax.Precision.HIGHEST


def carried_in(shard, axis, combine, identity):
    devices, mine = (lax.axis_size(axis), lax.axis_index(axis))
    everything = jax.tree.map(lambda part: lax.all_gather(part, axis), shard)
    start = jax.tree.map(
        lambda part, zero: jnp.broadcast_to(jnp.asarray(zero, part.dtype), part.shape),
        shard,
        identity,
    )

    def step(k, before):
        reached = k < mine
        new = combine(before, jax.tree.map(lambda part: part[k], everything))
        return jax.tree.map(lambda a, b: jnp.where(reached, a, b), new, before)

    return lax.fori_loop(0, devices, step, start)


def prefix_2(shard, axis, join, neutral):
    count = lax.axis_size(axis)
    place = lax.axis_index(axis)
    ahead = count - 1 - place
    gathered = jax.tree.map(
        lambda a, kind: lax.all_gather(a.astype(kind), axis),
        shard,
        jax.tree.map(lambda a: jnp.bfloat16 if a.dtype == jnp.float32 else a.dtype, shard),
    )
    state = jax.tree.map(lambda a, e: jnp.zeros_like(a) + jnp.asarray(e, a.dtype), shard, neutral)

    def one(step, state):
        source = count - 1 - step
        return join(
            state,
            jax.tree.map(
                lambda a, own: lax.dynamic_index_in_dim(a, source, 0, False).astype(own.dtype),
                gathered,
                shard,
            ),
        )

    return lax.fori_loop(0, ahead, one, state)


def product(left, right):
    return jnp.dot(left, right, preferred_element_type=jnp.float32)


def transposed(left, right):
    return jnp.dot(left.T, right, preferred_element_type=jnp.float32)


def rms_gain(token_rows, gain_row):
    return (
        token_rows
        * lax.rsqrt(jnp.mean(token_rows * token_rows, axis=-1, keepdims=True) + norm_eps)
        * gain_row
    )


def gated_norm(attended, gate_pre, head_gain):
    head_rows = attended.reshape(attended.shape[0], H, HV)
    gate_acts = jax.nn.silu(gate_pre.reshape(head_rows.shape))
    return (rms_gain(head_rows, head_gain) * gate_acts).reshape(attended.shape[0], H * HV)


def swiglu(gate_part, up_part):
    return jax.nn.silu(gate_part) * up_part


def block_scan(queries, key_rows, value_rows, log_decay):
    length = queries.shape[0]
    blocks = length // BLOCK
    key_scaling_factor = HK ** (-0.5)
    lower_mask = jnp.arange(BLOCK)[:, None] >= jnp.arange(BLOCK)[None, :]

    def advance(carried_state, pieces):
        query_part, key_part, value_portion, decay_part = pieces
        running = jnp.cumsum(decay_part, axis=0)
        block_count_total = running[-1]
        query_decayed = query_part * jnp.exp(running)
        key_dec = key_part * jnp.exp(-running)
        key_final_decay = key_part * jnp.exp(block_count_total[None] - running)
        scores = jnp.einsum("thk,shk->hts", query_decayed, key_dec, precision=highest_precision)
        scores = jnp.where(lower_mask[None], scores, 0.0)
        output_rows = jnp.einsum("hts,shv->thv", scores, value_portion, precision=highest_precision)
        output_rows = output_rows + jnp.einsum(
            "qse,seg->qsg", query_decayed, carried_state, precision=highest_precision
        )
        carried_state = jnp.exp(block_count_total)[:, :, None] * carried_state + jnp.einsum(
            "ufn,ufm->fnm", key_final_decay, value_portion, precision=highest_precision
        )
        return (carried_state, output_rows * key_scaling_factor)

    pieces = (
        queries.reshape(blocks, BLOCK, H, HK),
        key_rows.reshape(blocks, BLOCK, H, HK),
        value_rows.reshape(blocks, BLOCK, H, HV),
        log_decay.reshape(blocks, BLOCK, H, HK),
    )
    zero_state = jnp.zeros((H, HK, HV), jnp.float32)
    carried_state, output_rows = lax.scan(advance, zero_state, pieces)
    return (output_rows.reshape(length, H * HV), carried_state)


def combine_state(earlier, later):
    early_decay, early_state = earlier
    late_decay, late_state = later
    return (early_decay * late_decay, late_decay[:, :, None] * early_state + late_state)


def reduce_ffn(grads):
    sectioned = (
        lax.psum_scatter(grads[0], "seq", scatter_dimension=0, tiled=True),
        lax.psum_scatter(grads[1], "seq", scatter_dimension=0, tiled=True),
        lax.psum_scatter(grads[2], "seq", scatter_dimension=0, tiled=True),
        lax.psum_scatter(grads[3], "seq", scatter_dimension=1, tiled=True),
    )
    return (
        lax.psum_scatter(
            sectioned[0].astype(jnp.bfloat16), "fsdp", scatter_dimension=0, tiled=True
        ).astype(jnp.float32),
        lax.psum_scatter(
            sectioned[1].astype(jnp.bfloat16), "fsdp", scatter_dimension=0, tiled=True
        ).astype(jnp.float32),
        lax.psum_scatter(
            sectioned[2].astype(jnp.bfloat16), "fsdp", scatter_dimension=0, tiled=True
        ).astype(jnp.float32),
        lax.psum_scatter(
            sectioned[3].astype(jnp.bfloat16), "fsdp", scatter_dimension=1, tiled=True
        ).astype(jnp.float32),
    )


def reduce_attn(grads):
    sectioned = (
        lax.psum_scatter(grads[0], "seq", scatter_dimension=0, tiled=True),
        lax.psum_scatter(grads[1], "seq", scatter_dimension=0, tiled=True),
        lax.psum_scatter(grads[2], "seq", scatter_dimension=0, tiled=True),
        lax.psum_scatter(grads[3], "seq", scatter_dimension=0, tiled=True),
        lax.psum_scatter(grads[4], "seq", scatter_dimension=0, tiled=True),
        lax.psum_scatter(grads[5], "seq", scatter_dimension=0, tiled=True),
        lax.psum_scatter(grads[6], "seq", scatter_dimension=1, tiled=True),
        lax.psum_scatter(grads[7], "seq", scatter_dimension=0, tiled=True),
        lax.psum_scatter(grads[8], "seq", scatter_dimension=0, tiled=True),
        lax.psum_scatter(grads[9], "seq", scatter_dimension=0, tiled=True),
    )
    return (
        lax.psum_scatter(
            sectioned[0].astype(jnp.bfloat16), "fsdp", scatter_dimension=0, tiled=True
        ).astype(jnp.float32),
        lax.psum_scatter(
            sectioned[1].astype(jnp.bfloat16), "fsdp", scatter_dimension=0, tiled=True
        ).astype(jnp.float32),
        lax.psum_scatter(
            sectioned[2].astype(jnp.bfloat16), "fsdp", scatter_dimension=0, tiled=True
        ).astype(jnp.float32),
        lax.psum_scatter(
            sectioned[3].astype(jnp.bfloat16), "fsdp", scatter_dimension=0, tiled=True
        ).astype(jnp.float32),
        lax.psum_scatter(
            sectioned[4].astype(jnp.bfloat16), "fsdp", scatter_dimension=0, tiled=True
        ).astype(jnp.float32),
        lax.psum_scatter(
            sectioned[5].astype(jnp.bfloat16), "fsdp", scatter_dimension=0, tiled=True
        ).astype(jnp.float32),
        lax.psum_scatter(
            sectioned[6].astype(jnp.bfloat16), "fsdp", scatter_dimension=1, tiled=True
        ).astype(jnp.float32),
        lax.psum_scatter(
            sectioned[7].astype(jnp.bfloat16), "fsdp", scatter_dimension=0, tiled=True
        ).astype(jnp.float32),
        lax.psum_scatter(
            sectioned[8].astype(jnp.bfloat16), "fsdp", scatter_dimension=0, tiled=True
        ).astype(jnp.float32),
        lax.psum_scatter(
            sectioned[9].astype(jnp.bfloat16), "fsdp", scatter_dimension=0, tiled=True
        ).astype(jnp.float32),
    )


def on_device(
    block_input,
    attn_gain,
    query_weight,
    key_weight,
    value_weight,
    gate_weight,
    decay_down,
    decay_up,
    decay_bias,
    head_gain,
    out_weight,
    ffn_gain,
    ffn_gate,
    ffn_up,
    ffn_down,
    cotangent,
):
    token_rows = block_input[0]
    cot_rows = cotangent[0]
    attn_full = (
        lax.all_gather(attn_gain, "fsdp", axis=0, tiled=True),
        lax.all_gather(query_weight, "fsdp", axis=0, tiled=True),
        lax.all_gather(key_weight, "fsdp", axis=0, tiled=True),
        lax.all_gather(value_weight, "fsdp", axis=0, tiled=True),
        lax.all_gather(gate_weight, "fsdp", axis=0, tiled=True),
        lax.all_gather(decay_down, "fsdp", axis=0, tiled=True),
        lax.all_gather(decay_up, "fsdp", axis=1, tiled=True),
        lax.all_gather(decay_bias, "fsdp", axis=0, tiled=True),
        lax.all_gather(head_gain, "fsdp", axis=0, tiled=True),
        lax.all_gather(out_weight, "fsdp", axis=0, tiled=True),
    )
    ffn_full = (
        lax.all_gather(ffn_gain, "fsdp", axis=0, tiled=True),
        lax.all_gather(ffn_gate, "fsdp", axis=0, tiled=True),
        lax.all_gather(ffn_up, "fsdp", axis=0, tiled=True),
        lax.all_gather(ffn_down, "fsdp", axis=1, tiled=True),
    )
    (
        full_gain_one,
        full_query,
        full_key,
        full_value,
        full_gate,
        full_down,
        full_up,
        full_bias,
        full_head_gain,
        full_out,
    ) = attn_full
    full_gain_two, full_ffn_gate, full_ffn_up, full_ffn_down = ffn_full
    normed_one, norm_one_back = jax.vjp(rms_gain, token_rows, full_gain_one.astype(jnp.float32))
    hidden_one = normed_one.astype(jnp.bfloat16)
    queries = product(hidden_one, full_query).astype(jnp.bfloat16)
    key_rows = product(hidden_one, full_key).astype(jnp.bfloat16)
    value_rows = product(hidden_one, full_value).astype(jnp.bfloat16)
    gate_pre = product(hidden_one, full_gate)
    low_rank = product(hidden_one, full_down).astype(jnp.bfloat16)
    logits = product(low_rank, full_up) + full_bias.astype(jnp.float32)
    log_decay = jax.nn.log_sigmoid(logits) / logit_norm
    query_in = queries.astype(jnp.float32)
    key_in = key_rows.astype(jnp.float32)
    value_in = value_rows.astype(jnp.float32)
    local_out, scan_back, local_state = jax.vjp(
        block_scan, query_in, key_in, value_in, log_decay, has_aux=True
    )
    running = jnp.cumsum(log_decay, axis=0)
    block_decay = jnp.exp(running[-1]).reshape(H, HK)
    identity = (jnp.ones((H, HK), jnp.float32), jnp.zeros((H, HK, HV), jnp.float32))
    prefix = carried_in((block_decay, local_state), "seq", combine_state, identity)
    incoming_gradient = prefix[1]
    key_scaling_factor = HK ** (-0.5)
    grown = jnp.exp(running)
    query_expanded = (query_in * grown).reshape(-1, H, HK)
    cross_block_output = jnp.einsum(
        "qse,seg->qsg", query_expanded, incoming_gradient, precision=highest_precision
    )
    attended = local_out + key_scaling_factor * cross_block_output.reshape(-1, H * HV)
    gated, gated_back = jax.vjp(gated_norm, attended, gate_pre, full_head_gain.astype(jnp.float32))
    gated_low = gated.astype(jnp.bfloat16)
    residual = token_rows + product(gated_low, full_out)
    normed_two, norm_two_back = jax.vjp(rms_gain, residual, full_gain_two.astype(jnp.float32))
    hidden_two = normed_two.astype(jnp.bfloat16)
    ffn_gate_pre = product(hidden_two, full_ffn_gate)
    ffn_up_pre = product(hidden_two, full_ffn_up)
    mixed, mixed_back = jax.vjp(swiglu, ffn_gate_pre, ffn_up_pre)
    mixed_low = mixed.astype(jnp.bfloat16)
    block_output = residual + product(mixed_low, full_ffn_down)
    unused_gain, back_ffn_gate, back_ffn_up, back_ffn_down = ffn_full
    cot_low = cot_rows.astype(jnp.bfloat16)
    grad_ffn_down = transposed(mixed_low, cot_low)
    d_gate_part, d_up_part = mixed_back(product(cot_low, back_ffn_down.T))
    d_gate_low = d_gate_part.astype(jnp.bfloat16)
    d_up_low = d_up_part.astype(jnp.bfloat16)
    grad_ffn_gate = transposed(hidden_two, d_gate_low)
    grad_ffn_up = transposed(hidden_two, d_up_low)
    d_hidden_two = product(d_gate_low, back_ffn_gate.T) + product(d_up_low, back_ffn_up.T)
    d_residual_norm, grad_ffn_gain = norm_two_back(d_hidden_two)
    ffn_owned = reduce_ffn((grad_ffn_gain, grad_ffn_gate, grad_ffn_up, grad_ffn_down))
    d_residual = cot_rows + d_residual_norm
    (
        unused_one,
        back_query,
        back_key,
        back_value,
        back_gate,
        back_down,
        back_up,
        unused_bias,
        unused_head,
        back_out,
    ) = attn_full
    d_res_low = d_residual.astype(jnp.bfloat16)
    grad_out = transposed(gated_low, d_res_low)
    d_attended, d_gate_pre, grad_head_gain = gated_back(product(d_res_low, back_out.T))
    head_gradients = d_attended.reshape(-1, H, HV)
    query_backward_pull = key_scaling_factor * jnp.einsum(
        "ifw,ifc->fwc", query_expanded, head_gradients, precision=highest_precision
    )
    later = prefix_2((block_decay, query_backward_pull), "seq", combine_state, identity)
    later_gradient = later[1]
    d_local_query, d_local_key, d_local_value, unused_decay = scan_back(d_attended)
    to_end = jnp.exp(running[-1][None] - running)
    later_key_rows = (key_in * to_end).reshape(-1, H, HK)
    head_value_rows = value_in.reshape(-1, H, HV)
    cross_block_query = jnp.einsum(
        "ogw,gsw->ogs", head_gradients, incoming_gradient, precision=highest_precision
    ).reshape(-1, H * HK)
    d_queries = d_local_query + key_scaling_factor * grown * cross_block_query
    cross_block_key = jnp.einsum(
        "ogw,gsw->ogs", head_value_rows, later_gradient, precision=highest_precision
    ).reshape(-1, H * HK)
    d_keys = d_local_key + to_end * cross_block_key
    cross_block_value = jnp.einsum(
        "qse,seg->qsg", later_key_rows, later_gradient, precision=highest_precision
    ).reshape(-1, H * HV)
    d_values = d_local_value + cross_block_value
    outgoing = block_decay[:, :, None] * incoming_gradient + local_state
    tail_term = jnp.sum(later_gradient * outgoing, axis=2).reshape(H * HK)
    through = query_in * d_queries - key_in * d_keys
    d_log_decay = jnp.flip(jnp.cumsum(jnp.flip(through, 0), axis=0), 0) + tail_term[None]
    d_logits = d_log_decay * jax.nn.sigmoid(-logits) / logit_norm
    grad_decay_bias = jnp.sum(d_logits, axis=0)
    d_logits_low = d_logits.astype(jnp.bfloat16)
    grad_decay_up = transposed(low_rank, d_logits_low)
    d_low_rank = product(d_logits_low, back_up.T).astype(jnp.bfloat16)
    grad_decay_down = transposed(hidden_one, d_low_rank)
    d_query_low = d_queries.astype(jnp.bfloat16)
    d_key_low = d_keys.astype(jnp.bfloat16)
    d_value_low = d_values.astype(jnp.bfloat16)
    d_gate_one = d_gate_pre.astype(jnp.bfloat16)
    grad_query = transposed(hidden_one, d_query_low)
    grad_key = transposed(hidden_one, d_key_low)
    grad_value = transposed(hidden_one, d_value_low)
    grad_gate = transposed(hidden_one, d_gate_one)
    d_hidden_one = (
        product(d_query_low, back_query.T)
        + product(d_key_low, back_key.T)
        + product(d_value_low, back_value.T)
        + product(d_gate_one, back_gate.T)
        + product(d_low_rank, back_down.T)
    )
    d_input_norm, grad_attn_gain = norm_one_back(d_hidden_one)
    input_grad = d_residual + d_input_norm
    attn_owned = reduce_attn(
        (
            grad_attn_gain,
            grad_query,
            grad_key,
            grad_value,
            grad_gate,
            grad_decay_down,
            grad_decay_up,
            grad_decay_bias,
            grad_head_gain,
            grad_out,
        )
    )
    (
        own_attn_gain,
        own_query,
        own_key,
        own_value,
        own_gate,
        own_down,
        own_up,
        own_bias,
        own_head_gain,
        own_out,
    ) = attn_owned
    own_ffn_gain, own_ffn_gate, own_ffn_up, own_ffn_down = ffn_owned
    return (
        block_output[None],
        input_grad[None],
        own_attn_gain,
        own_query,
        own_key,
        own_value,
        own_gate,
        own_down,
        own_up,
        own_bias,
        own_head_gain,
        own_out,
        own_ffn_gain,
        own_ffn_gate,
        own_ffn_up,
        own_ffn_down,
    )


def solution(mesh):
    return jax.shard_map(
        on_device,
        mesh=mesh,
        in_specs=(
            P("fsdp", "seq", None),
            P("fsdp"),
            P("fsdp", None),
            P("fsdp", None),
            P("fsdp", None),
            P("fsdp", None),
            P("fsdp", None),
            P(None, "fsdp"),
            P("fsdp"),
            P("fsdp"),
            P("fsdp", None),
            P("fsdp"),
            P("fsdp", None),
            P("fsdp", None),
            P(None, "fsdp"),
            P("fsdp", "seq", None),
        ),
        out_specs=(
            P("fsdp", "seq", None),
            P("fsdp", "seq", None),
            P(("seq", "fsdp")),
            P(("seq", "fsdp"), None),
            P(("seq", "fsdp"), None),
            P(("seq", "fsdp"), None),
            P(("seq", "fsdp"), None),
            P(("seq", "fsdp"), None),
            P(None, ("seq", "fsdp")),
            P(("seq", "fsdp")),
            P(("seq", "fsdp")),
            P(("seq", "fsdp"), None),
            P(("seq", "fsdp")),
            P(("seq", "fsdp"), None),
            P(("seq", "fsdp"), None),
            P(None, ("seq", "fsdp")),
        ),
        check_vma=False,
    )
```

profile of v0, /device:TPU:0, one launch (start us, length us, event | category | flops | bytes accessed | tf_op | source)
XLA Modules:
  0.0 1458.0 jit_solution(5585916566595208693)
XLA Ops:
  10.2 12.8 all-gather.3
  23.6 7.9 all-gather.2
  33.3 13.3 all_gather.62
  46.6 12.2 all_gather.63
  62.2 7.6 all-gather.20.cloned.1.call-done
  72.1 44.3 %all-gather.18.cloned.1.call-done = bf16[1024,1024]{1,0:T(8,128)(2,1)} async-done(((bf16[256,1024]{1,0:T(8,128)(2,1)}), bf16[1024,1024]{1,0:T(8,128)(2,1)}) %all-gather.18.cloned.1.call-update) | async-done | bytes 2097168 | tf_op jit(solution)/shard_map/all_gather | solution.py:220
  121.3 8.6 while.82
  135.3 10.4 all-reduce
  145.7 9.3 all-gather.4
  155.7 8.7 all_gather.78
  164.4 9.0 all_gather.68
  175.8 3.9 copy.148
  179.7 20.1 %all-gather.32.cloned.1.call-done = f32[32,128,256]{2,1,0:T(8,128)} async-done(((f32[4,128,256]{2,1,0:T(8,128)}), f32[32,128,256]{2,1,0:T(8,128)}) %all-gather.32.cloned.1.call-update) | async-done | bytes 4194320 | tf_op jit(solution)/shard_map/all_gather | solution.py:19
  199.8 10.3 while.83
  215.4 31.5 %all-gather.24.cloned.1.call-done = bf16[1024,1024]{1,0:T(8,128)(2,1)} async-done(((bf16[256,1024]{1,0:T(8,128)(2,1)}), bf16[1024,1024]{1,0:T(8,128)(2,1)}) %all-gather.24.cloned.1.call-update) | async-done | bytes 2097168 | tf_op jit(solution)/shard_map/all_gather | solution.py:226
  249.3 104.7 %all-gather.26.cloned.1.call-done = bf16[1024,2816]{1,0:T(8,128)(2,1)} async-done(((bf16[256,2816]{1,0:T(8,128)(2,1)}), bf16[1024,2816]{1,0:T(8,128)(2,1)}) %all-gather.26.cloned.1.call-update) | async-done | bytes 5767184 | tf_op jit(solution)/shard_map/all_gather | solution.py:230
  354.0 4.6 fusion.153
  358.7 101.9 %all-gather.28.cloned.1.call-done = bf16[1024,2816]{1,0:T(8,128)(2,1)} async-done(((bf16[256,2816]{1,0:T(8,128)(2,1)}), bf16[1024,2816]{1,0:T(8,128)(2,1)}) %all-gather.28.cloned.1.call-update) | async-done | bytes 5767184 | tf_op jit(solution)/shard_map/all_gather | solution.py:231
  460.6 4.7 fusion.154
  465.3 101.4 %all-gather.30.cloned.1.call-done = bf16[2816,1024]{1,0:T(8,128)(2,1)} async-done(((bf16[2816,256]{1,0:T(8,128)(2,1)}), bf16[2816,1024]{1,0:T(8,128)(2,1)}) %all-gather.30.cloned.1.call-update) | async-done | bytes 5767184 | tf_op jit(solution)/shard_map/all_gather | solution.py:232
  566.7 6.8 multiply_convert_fusion
  573.5 5.2 fusion.155
  596.3 12.3 while.84
  612.3 5.8 all-gather.34.cloned.1.call-done
  618.1 8.1 while.81
  663.2 5.9 fusion.149
  670.2 5.9 fusion.158
  677.2 5.9 fusion.159
  684.8 24.2 %reduce-scatter.45.cloned.1.call-done = f32[128,16]{0,1:T(8,128)} async-done(((f32[1024,16]{0,1:T(8,128)}), f32[128,16]{0,1:T(8,128)}) %reduce-scatter.45.cloned.1.call-update) | async-done | bytes 8208 | tf_op jit(solution)/shard_map/reduce_scatter | solution.py:156
  710.4 53.0 %reduce-scatter.41.cloned.1.call-done = f32[128,1024]{1,0:T(8,128)} async-done(((f32[1024,1024]{1,0:T(8,128)}), f32[128,1024]{1,0:T(8,128)}) %reduce-scatter.41.cloned.1.call-update) | async-done | bytes 524304 | tf_op jit(solution)/shard_map/reduce_scatter | solution.py:155
  765.3 52.6 %reduce-scatter.47.cloned.1.call-done = f32[128,1024]{1,0:T(8,128)} async-done(((f32[1024,1024]{1,0:T(8,128)}), f32[128,1024]{1,0:T(8,128)}) %reduce-scatter.47.cloned.1.call-update) | async-done | bytes 524304 | tf_op jit(solution)/shard_map/reduce_scatter | solution.py:160
  819.7 42.4 %reduce-scatter.29.cloned.1.call-done = f32[128,512]{1,0:T(8,128)} async-done(((f32[1024,512]{1,0:T(8,128)}), f32[128,512]{1,0:T(8,128)}) %reduce-scatter.29.cloned.1.call-update) | async-done | bytes 262160 | tf_op jit(solution)/shard_map/reduce_scatter | solution.py:152
  863.8 42.6 %reduce-scatter.33.cloned.1.call-done = f32[128,512]{1,0:T(8,128)} async-done(((f32[1024,512]{1,0:T(8,128)}), f32[128,512]{1,0:T(8,128)}) %reduce-scatter.33.cloned.1.call-update) | async-done | bytes 262160 | tf_op jit(solution)/shard_map/reduce_scatter | solution.py:153
  908.1 52.7 %reduce-scatter.37.cloned.1.call-done = f32[128,1024]{1,0:T(8,128)} async-done(((f32[1024,1024]{1,0:T(8,128)}), f32[128,1024]{1,0:T(8,128)}) %reduce-scatter.37.cloned.1.call-update) | async-done | bytes 524304 | tf_op jit(solution)/shard_map/reduce_scatter | solution.py:154
  962.7 88.4 %reduce-scatter.59.cloned.1.call-done = f32[2816,128]{1,0:T(8,128)} async-done(((f32[2816,1024]{1,0:T(8,128)}), f32[2816,128]{1,0:T(8,128)}) %reduce-scatter.59.cloned.1.call-update) | async-done | bytes 1441808 | tf_op jit(solution)/shard_map/reduce_scatter | solution.py:131
  1053.7 88.0 %reduce-scatter.51.cloned.1.call-done = f32[128,2816]{1,0:T(8,128)} async-done(((f32[1024,2816]{1,0:T(8,128)}), f32[128,2816]{1,0:T(8,128)}) %reduce-scatter.51.cloned.1.call-update) | async-done | bytes 1441808 | tf_op jit(solution)/shard_map/reduce_scatter | solution.py:129
  1154.0 5.8 fusion.89
  1162.3 69.9 %reduce-scatter.55.cloned.1.call-done = f32[128,2816]{1,0:T(8,128)} async-done(((f32[1024,2816]{1,0:T(8,128)}), f32[128,2816]{1,0:T(8,128)}) %reduce-scatter.55.cloned.1.call-update) | async-done | bytes 1441808 | tf_op jit(solution)/shard_map/reduce_scatter | solution.py:130
  1237.7 23.3 %all-reduce.9 = (bf16[1024]{0:T(1024)(128)(2,1)S(1)}, bf16[512]{0:T(512)(128)(2,1)S(1)}, bf16[256]{0:T(256)(128)(2,1)S(1)}, bf16[1024]{0:T(1024)(128)(2,1)S(1)}) all-reduce(f32[1024]{0:T(1024)S(1)} %get-tuple-element.982, f32[512]{0:T(512)S(1)} %copy-done.76, ...), channel_id=4, replica_groups=mesh['seq'=8,'fsdp'=4] {'seq'}, use_global_device_ids=true, to_apply=%region_19.20.clone | all-reduce | flops 2816 | bytes 16896
  1261.3 11.3 all-reduce.10
  1278.1 17.4 %reduce-scatter.43.cloned.1.call-done = bf16[32,1024]{1,0:T(8,128)(2,1)} async-done(((bf16[128,1024]{1,0:T(8,128)(2,1)}), bf16[32,1024]{1,0:T(8,128)(2,1)}) %reduce-scatter.43.cloned.1.call-update) | async-done | bytes 65552 | tf_op jit(solution)/shard_map/reduce_scatter | solution.py:175
  1297.0 18.9 %reduce-scatter.49.cloned.1.call-done = bf16[32,1024]{1,0:T(8,128)(2,1)} async-done(((bf16[128,1024]{1,0:T(8,128)(2,1)}), bf16[32,1024]{1,0:T(8,128)(2,1)}) %reduce-scatter.49.cloned.1.call-update) | async-done | bytes 65552 | tf_op jit(solution)/shard_map/reduce_scatter | solution.py:190
  1317.4 19.0 %reduce-scatter.31.cloned.1.call-done = bf16[32,512]{1,0:T(8,128)(2,1)} async-done(((bf16[128,512]{1,0:T(8,128)(2,1)}), bf16[32,512]{1,0:T(8,128)(2,1)}) %reduce-scatter.31.cloned.1.call-update) | async-done | bytes 32784 | tf_op jit(solution)/shard_map/reduce_scatter | solution.py:166
  1337.8 18.4 %reduce-scatter.35.cloned.1.call-done = bf16[32,512]{1,0:T(8,128)(2,1)} async-done(((bf16[128,512]{1,0:T(8,128)(2,1)}), bf16[32,512]{1,0:T(8,128)(2,1)}) %reduce-scatter.35.cloned.1.call-update) | async-done | bytes 32784 | tf_op jit(solution)/shard_map/reduce_scatter | solution.py:169
  1357.5 19.5 %reduce-scatter.39.cloned.1.call-done = bf16[32,1024]{1,0:T(8,128)(2,1)} async-done(((bf16[128,1024]{1,0:T(8,128)(2,1)}), bf16[32,1024]{1,0:T(8,128)(2,1)}) %reduce-scatter.39.cloned.1.call-update) | async-done | bytes 65552 | tf_op jit(solution)/shard_map/reduce_scatter | solution.py:172
  1378.5 22.0 %reduce-scatter.67.cloned.1.call-done = bf16[32,2816]{1,0:T(8,128)(2,1)} async-done(((bf16[128,2816]{1,0:T(8,128)(2,1)}), bf16[32,2816]{1,0:T(8,128)(2,1)}) %reduce-scatter.67.cloned.1.call-update) | async-done | bytes 180240
  1402.9 22.0 %reduce-scatter.53.cloned.1.call-done = bf16[32,2816]{1,0:T(8,128)(2,1)} async-done(((bf16[128,2816]{1,0:T(8,128)(2,1)}), bf16[32,2816]{1,0:T(8,128)(2,1)}) %reduce-scatter.53.cloned.1.call-update) | async-done | bytes 180240 | tf_op jit(solution)/shard_map/reduce_scatter | solution.py:137
  1426.6 22.5 %reduce-scatter.57.cloned.1.call-done = bf16[32,2816]{1,0:T(8,128)(2,1)} async-done(((bf16[128,2816]{1,0:T(8,128)(2,1)}), bf16[32,2816]{1,0:T(8,128)(2,1)}) %reduce-scatter.57.cloned.1.call-update) | async-done | bytes 180240 | tf_op jit(solution)/shard_map/reduce_scatter | solution.py:140
  (502 shorter events, 178.5 us)
Async XLA Ops:
  7.2 51.6 %copy-start.3 = (f32[1,128,1024]{2,1,0:T(8,128)S(1)}, f32[1,128,1024]{2,1,0:T(8,128)}, u32[]{:S(2)}) copy-start(f32[1,128,1024]{2,1,0:T(8,128)} %param.24) | copy-start | bytes 1572868
  7.2 26.1 %copy-start.77 = (bf16[256,16]{0,1:T(8,128)(2,1)S(1)}, bf16[256,16]{0,1:T(8,128)(2,1)}, u32[]{:S(2)}) copy-start(bf16[256,16]{0,1:T(8,128)(2,1)} %param.30) | copy-start | bytes 24580
  7.2 39.4 %copy-start.81 = (bf16[16,128]{1,0:T(8,128)(2,1)S(1)}, bf16[16,128]{1,0:T(8,128)(2,1)}, u32[]{:S(2)}) copy-start(bf16[16,128]{1,0:T(8,128)(2,1)} %param.31) | copy-start | bytes 12292
  7.2 53.3 %all-gather.16.cloned.1.call-start = ((), (), s32[]{:S(2)}) async-start(), calls=%async_computation.20 | async-start | bytes 1310720 | tf_op jit(solution)/shard_map/all_gather | solution.py:219
  7.9 61.8 %all-gather.20.cloned.1.call-start = ((), (), s32[]{:S(2)}) async-start(), calls=%async_computation.22 | async-start | bytes 1310720 | tf_op jit(solution)/shard_map/all_gather | solution.py:218
  8.7 107.7 %all-gather.18.cloned.1.call-start = ((), (), s32[]{:S(2)}) async-start(), calls=%async_computation.21 | async-start | bytes 2621440 | tf_op jit(solution)/shard_map/all_gather | solution.py:220
  9.4 166.4 %all-gather.22.cloned.1.call-start = ((), (), s32[]{:S(2)}) async-start(), calls=%async_computation.23 | async-start | bytes 2621440 | tf_op jit(solution)/shard_map/all_gather | solution.py:221
  10.0 189.8 %all-gather.32.cloned.1.call-start = ((), (), s32[]{:S(2)}) async-start(), calls=%async_computation.44 | async-start | bytes 4718592 | tf_op jit(solution)/shard_map/all_gather | solution.py:19
  33.3 140.1 %copy-start.78 = (f32[128]{0:T(128)}, f32[128]{0:T(128)S(1)}, u32[]{:S(2)}) copy-start(f32[128]{0:T(128)S(1)} %fusion.141) | copy-start | bytes 1540
  46.6 13.5 copy-start.71
  58.9 57.6 %copy-start.4 = (bf16[128,1024]{1,0:T(8,128)(2,1)}, bf16[128,1024]{1,0:T(8,128)(2,1)S(1)}, u32[]{:S(2)}) copy-start(bf16[128,1024]{1,0:T(8,128)(2,1)S(1)} %multiply_convert_fusion.5) | copy-start | bytes 786436
  60.5 94.6 %copy-start.12 = (f32[128,512]{1,0:T(8,128)}, f32[128,512]{1,0:T(8,128)S(1)}, u32[]{:S(2)}) copy-start(f32[128,512]{1,0:T(8,128)S(1)} %reduce_window_sum.34) | copy-start | bytes 786436
  72.0 49.3 %copy-start.43 = (f32[128,512]{1,0:T(8,128)}, f32[128,512]{1,0:T(8,128)S(1)}, u32[]{:S(2)}) copy-start(f32[128,512]{1,0:T(8,128)S(1)} %get-tuple-element.1116) | copy-start | bytes 786436
  130.8 116.1 %all-gather.24.cloned.1.call-start = ((), (), s32[]{:S(2)}) async-start(), calls=%async_computation.24 | async-start | bytes 2621440 | tf_op jit(solution)/shard_map/all_gather | solution.py:226
  131.4 14.3 copy-start.86
  131.4 222.6 %all-gather.26.cloned.1.call-start = ((), (), s32[]{:S(2)}) async-start(), calls=%async_computation.25 | async-start | bytes 7208960 | tf_op jit(solution)/shard_map/all_gather | solution.py:230
  132.2 41.4 %copy-start.68 = (f32[128,512]{1,0:T(8,128)S(1)}, f32[128,512]{1,0:T(8,128)}, u32[]{:S(2)}) copy-start(f32[128,512]{1,0:T(8,128)} %get-tuple-element.1115) | copy-start | bytes 786436
  132.2 328.4 %all-gather.28.cloned.1.call-start = ((), (), s32[]{:S(2)}) async-start(), calls=%async_computation.26 | async-start | bytes 7208960 | tf_op jit(solution)/shard_map/all_gather | solution.py:231
  132.9 433.8 %all-gather.30.cloned.1.call-start = ((), (), s32[]{:S(2)}) async-start(), calls=%async_computation.27 | async-start | bytes 7208960 | tf_op jit(solution)/shard_map/all_gather | solution.py:232
  133.7 484.3 %all-gather.34.cloned.1.call-start = ((), (), s32[]{:S(2)}) async-start(), calls=%async_computation.45 | async-start | bytes 2359296 | tf_op jit(solution)/shard_map/all_gather | solution.py:39
  173.5 38.7 %copy-start.15 = (bf16[1,128,1024]{2,1,0:T(8,128)(2,1)}, bf16[1,128,1024]{2,1,0:T(8,128)(2,1)S(1)}, u32[]{:S(2)}) copy-start(bf16[1,128,1024]{2,1,0:T(8,128)(2,1)S(1)} %multiply_convert_fusion.4) | copy-start | bytes 786436
  173.7 36.5 %copy-start.41 = (f32[128,512]{0,1:T(8,128)}, f32[128,512]{0,1:T(8,128)S(1)}, u32[]{:S(2)}) copy-start(f32[128,512]{0,1:T(8,128)S(1)} %copy.227) | copy-start | bytes 786436
  591.9 91.2 %reduce-scatter.63.cloned.1.call-start = ((), (), s32[]{:S(2)}) async-start(), calls=%async_computation.47 | async-start | bytes 294912
  641.1 67.8 %reduce-scatter.45.cloned.1.call-start = ((), (), s32[]{:S(2)}) async-start(), calls=%async_computation.36 | async-start | bytes 73728 | tf_op jit(solution)/shard_map/reduce_scatter | solution.py:156
  642.0 121.4 %reduce-scatter.41.cloned.1.call-start = ((), (), s32[]{:S(2)}) async-start(), calls=%async_computation.34 | async-start | bytes 4718592 | tf_op jit(solution)/shard_map/reduce_scatter | solution.py:155
  645.8 172.1 %reduce-scatter.47.cloned.1.call-start = ((), (), s32[]{:S(2)}) async-start(), calls=%async_computation.37 | async-start | bytes 4718592 | tf_op jit(solution)/shard_map/reduce_scatter | solution.py:160
  649.5 212.6 %reduce-scatter.29.cloned.1.call-start = ((), (), s32[]{:S(2)}) async-start(), calls=%async_computation.28 | async-start | bytes 2359296 | tf_op jit(solution)/shard_map/reduce_scatter | solution.py:152
  654.5 251.9 %reduce-scatter.33.cloned.1.call-start = ((), (), s32[]{:S(2)}) async-start(), calls=%async_computation.30 | async-start | bytes 2359296 | tf_op jit(solution)/shard_map/reduce_scatter | solution.py:153
  656.5 304.4 %reduce-scatter.37.cloned.1.call-start = ((), (), s32[]{:S(2)}) async-start(), calls=%async_computation.32 | async-start | bytes 4718592 | tf_op jit(solution)/shard_map/reduce_scatter | solution.py:154
  662.0 389.1 %reduce-scatter.59.cloned.1.call-start = ((), (), s32[]{:S(2)}) async-start(), calls=%async_computation.43 | async-start | bytes 12976128 | tf_op jit(solution)/shard_map/reduce_scatter | solution.py:131
  669.1 472.6 %reduce-scatter.51.cloned.1.call-start = ((), (), s32[]{:S(2)}) async-start(), calls=%async_computation.39 | async-start | bytes 12976128 | tf_op jit(solution)/shard_map/reduce_scatter | solution.py:129
  676.1 556.1 %reduce-scatter.55.cloned.1.call-start = ((), (), s32[]{:S(2)}) async-start(), calls=%async_computation.41 | async-start | bytes 12976128 | tf_op jit(solution)/shard_map/reduce_scatter | solution.py:130
  683.1 592.3 %reduce-scatter.65.cloned.1.call-start = ((), (), s32[]{:S(2)}) async-start(), calls=%async_computation.48 | async-start | bytes 20480
  684.7 592.0 %reduce-scatter.61.cloned.1.call-start = ((), (), s32[]{:S(2)}) async-start(), calls=%async_computation.46 | async-start | bytes 40960
  710.4 585.1 %reduce-scatter.43.cloned.1.call-start = ((), (), s32[]{:S(2)}) async-start(), calls=%async_computation.35 | async-start | bytes 327680 | tf_op jit(solution)/shard_map/reduce_scatter | solution.py:175
  765.2 550.6 %reduce-scatter.49.cloned.1.call-start = ((), (), s32[]{:S(2)}) async-start(), calls=%async_computation.38 | async-start | bytes 327680 | tf_op jit(solution)/shard_map/reduce_scatter | solution.py:190
  819.6 516.7 %reduce-scatter.31.cloned.1.call-start = ((), (), s32[]{:S(2)}) async-start(), calls=%async_computation.29 | async-start | bytes 163840 | tf_op jit(solution)/shard_map/reduce_scatter | solution.py:166
  863.8 492.4 %reduce-scatter.35.cloned.1.call-start = ((), (), s32[]{:S(2)}) async-start(), calls=%async_computation.31 | async-start | bytes 163840 | tf_op jit(solution)/shard_map/reduce_scatter | solution.py:169
  908.1 468.9 %reduce-scatter.39.cloned.1.call-start = ((), (), s32[]{:S(2)}) async-start(), calls=%async_computation.33 | async-start | bytes 327680 | tf_op jit(solution)/shard_map/reduce_scatter | solution.py:172
  962.6 437.9 %reduce-scatter.67.cloned.1.call-start = ((), (), s32[]{:S(2)}) async-start(), calls=%async_computation.49 | async-start | bytes 901120
  1053.7 90.4 %copy-start.87 = (u32[32]{0:T(128)S(1)}, u32[32]{0:T(128)}, u32[]{:S(2)}) copy-start(u32[32]{0:T(128)} %constant.227) | copy-start | bytes 388
  1053.7 96.2 %copy-start.22 = (bf16[1024,512]{1,0:T(8,128)(2,1)S(1)}, bf16[1024,512]{1,0:T(8,128)(2,1)}, u32[]{:S(2)}) copy-start(bf16[1024,512]{1,0:T(8,128)(2,1)} %all-gather.20.cloned.1.call-done) | copy-start | bytes 3145732
  1053.7 371.2 %reduce-scatter.53.cloned.1.call-start = ((), (), s32[]{:S(2)}) async-start(), calls=%async_computation.40 | async-start | bytes 901120 | tf_op jit(solution)/shard_map/reduce_scatter | solution.py:137
  1144.0 305.0 %reduce-scatter.57.cloned.1.call-start = ((), (), s32[]{:S(2)}) async-start(), calls=%async_computation.42 | async-start | bytes 901120 | tf_op jit(solution)/shard_map/reduce_scatter | solution.py:140
  1159.9 74.7 %copy-start.6 = (bf16[1024,1024]{1,0:T(8,128)(2,1)S(1)}, bf16[1024,1024]{1,0:T(8,128)(2,1)}, u32[]{:S(2)}) copy-start(bf16[1024,1024]{1,0:T(8,128)(2,1)} %all-gather.18.cloned.1.call-done) | copy-start | bytes 6291460
  1159.9 74.7 %copy-start.44 = (f32[16,8,4,256]{3,1,2,0:T(8,128)S(1)}, f32[16,8,4,256]{3,1,2,0:T(8,128)}, u32[]{:S(2)}) copy-start(f32[16,8,4,256]{3,1,2,0:T(8,128)} %copy.232) | copy-start | bytes 1572868
  1236.7 37.7 %copy-start.84 = (f32[128]{0:T(128)S(1)}, f32[128]{0:T(128)}, u32[]{:S(2)}) copy-start(f32[128]{0:T(128)} %copy-done.83) | copy-start | bytes 1540
  1236.7 37.7 %copy-start.11 = (f32[128,1024]{1,0:T(8,128)S(1)}, f32[128,1024]{1,0:T(8,128)}, u32[]{:S(2)}) copy-start(f32[128,1024]{1,0:T(8,128)} %copy-done.9) | copy-start | bytes 1572868
  (94 other events, 230.9 us)
Sparse Core Ops, SparseCore 0:
  9.6 31.0 all-gather.15
  42.2 27.5 all-gather.19
  71.4 45.0 all-gather.17
  117.9 44.7 all-gather.21
  164.4 35.3 all-gather.31
  201.3 45.6 all-gather.23
  248.5 105.4 all-gather.25
  355.6 104.9 all-gather.27
  462.2 104.4 all-gather.29
  592.0 25.9 all-gather.33
  641.3 32.7 reduce-scatter.62
  677.5 31.3 reduce-scatter.44
  712.3 51.1 reduce-scatter.40
  766.7 51.1 reduce-scatter.46
  821.0 41.1 reduce-scatter.28
  865.3 41.1 reduce-scatter.32
  909.6 51.1 reduce-scatter.36
  964.2 86.8 reduce-scatter.58
  1054.6 87.0 reduce-scatter.50
  1145.1 87.0 reduce-scatter.54
  1235.0 19.2 reduce-scatter.64
  1257.1 17.3 reduce-scatter.60
  1277.3 18.1 reduce-scatter.42
  1297.6 18.2 reduce-scatter.48
  1318.7 17.6 reduce-scatter.30
  1338.5 17.6 reduce-scatter.34
  1358.8 18.1 reduce-scatter.38
  1379.3 21.2 reduce-scatter.66
  1402.9 21.9 reduce-scatter.52
  1427.0 21.9 reduce-scatter.56
where the time goes:
time: 1470 us; the launch traced here: 1460 us
  waiting for transfers between devices  1100 us (75%)
  blocking collectives  118 us (8%)
  matrix products  103 us (7%)
  other arithmetic  62.5 us (4%)
  local copies, waits for them, and re-layouts  54.1 us (4%)
  between operations  20.5 us (1%)
    all_gather x1, waiting for transfers between devices, on_device(): lax.all_gather(ffn_gate, 'fsdp', axis=0, tiled=True)  105 us
    all_gather x1, waiting for transfers between devices, on_device(): lax.all_gather(ffn_up, 'fsdp', axis=0, tiled=True)  102 us
    all_gather x1, waiting for transfers between devices, on_device(): lax.all_gather(ffn_down, 'fsdp', axis=1, tiled=True)  101 us
    reduce_scatter x1, waiting for transfers between devices, reduce_ffn(): lax.psum_scatter(grads[3], 'seq', scatter_dimension=1, tiled=True)  88.4 us
    reduce_scatter x1, waiting for transfers between devices, reduce_ffn(): lax.psum_scatter(grads[1], 'seq', scatter_dimension=0, tiled=True)  88 us
    reduce_scatter x1, waiting for transfers between devices, reduce_ffn(): lax.psum_scatter(grads[2], 'seq', scatter_dimension=0, tiled=True)  69.9 us
    reduce_scatter x1, waiting for transfers between devices, reduce_attn(): lax.psum_scatter(grads[4], 'seq', scatter_dimension=0, tiled=True)  53 us
    reduce_scatter x1, waiting for transfers between devices, reduce_attn(): lax.psum_scatter(grads[3], 'seq', scatter_dimension=0, tiled=True)  52.7 us
  transfers between devices with their start and end apart: 30, of which 25 were waited for; matrix products, arithmetic and copies ran while one was open for 11% of the time, Pallas kernels for 0%

commit v1 on v0

v1 whole, which is shorter than its diff:
```python
import jax
import jax.numpy as jnp
from jax import lax
from jax.sharding import PartitionSpec as P

HK = 128
HV = 256
BLOCK = 64


norm_eps = 1e-06
logit_norm = 16.0
exact = lax.Precision.HIGHEST
fine = lax.Precision.HIGH
low = jnp.bfloat16
wide = jnp.float32


def product(left, right):
    return jnp.dot(left, right, preferred_element_type=wide)


def transposed(left, right):
    return lax.dot_general(left, right, (((0,), (0,)), ((), ())), preferred_element_type=wide)


def against(left, right):
    return lax.dot_general(left, right, (((1,), (1,)), ((), ())), preferred_element_type=wide)


def fine_dot(spec, left, right):
    return jnp.einsum(spec, left, right, precision=fine, preferred_element_type=wide)


def rms_gain(token_rows, gain_row):
    return (
        token_rows
        * lax.rsqrt(jnp.mean(token_rows * token_rows, axis=-1, keepdims=True) + norm_eps)
        * gain_row
    )


def gated_norm(attended, gate_pre, head_gain):
    return rms_gain(attended, head_gain) * jax.nn.silu(gate_pre)


def swiglu(gate_part, up_part):
    return jax.nn.silu(gate_part) * up_part


def exchange(pieces):
    return lax.all_to_all(pieces, "fsdp", 0, 0)


def gather_rows(rows):
    return lax.all_gather(rows, "fsdp", axis=0, tiled=True)


def scatter_rows(rows):
    return lax.psum_scatter(rows.astype(low), "fsdp", scatter_dimension=0, tiled=True).astype(wide)


def column_owned(weights, parts, si, shards):
    rows = weights[0].shape[0] // shards
    cuts = [
        lax.dynamic_slice_in_dim(w, si * rows, rows, 0).reshape(rows, parts, -1) for w in weights
    ]
    sent = jnp.concatenate(cuts, axis=2).transpose(1, 0, 2)
    got = lax.all_gather(exchange(sent), "seq")
    return got.transpose(1, 0, 2, 3).reshape(parts * shards * rows, -1)


def owned_columns(grads, parts):
    section = lax.psum_scatter(grads.astype(low), "seq", scatter_dimension=0, tiled=True)
    rows = section.shape[0] // parts
    return exchange(section.reshape(parts, rows, -1))


def across(pieces):
    rows = pieces.shape[1]
    return pieces.transpose(1, 0, 2).reshape(rows, -1).astype(wide)


def on_device(
    block_input,
    attn_gain,
    query_weight,
    key_weight,
    value_weight,
    gate_weight,
    decay_down,
    decay_up,
    decay_bias,
    head_gain,
    out_weight,
    ffn_gain,
    ffn_gate,
    ffn_up,
    ffn_down,
    cotangent,
):
    shards, parts = lax.axis_size("seq"), lax.axis_size("fsdp")
    si = lax.axis_index("seq")
    x = block_input[0]
    cot_rows = cotangent[0]
    length, width = x.shape
    blocks = length // BLOCK
    scale = HK ** (-0.5)

    small = lax.all_gather(
        jnp.concatenate([attn_gain, ffn_gain, head_gain, decay_down.reshape(-1)]), "fsdp"
    )
    own = attn_gain.shape[0]
    own_head = head_gain.shape[0]
    gain_one = small[:, :own].reshape(-1).astype(wide)
    gain_two = small[:, own : 2 * own].reshape(-1).astype(wide)
    gain_head = small[:, 2 * own : 2 * own + own_head].reshape(-1).astype(wide)
    down_full = small[:, 2 * own + own_head :].reshape(width, -1)
    rank = down_full.shape[1]

    normed_one, norm_one_back = jax.vjp(rms_gain, x, gain_one)
    hidden_one = gather_rows(normed_one.astype(low))
    attn_w = column_owned(
        (query_weight, key_weight, value_weight, gate_weight), parts, si, shards
    )
    cot_low = gather_rows(cot_rows.astype(low))
    ffn_w = column_owned((ffn_gate, ffn_up), parts, si, shards)
    ff = ffn_w.shape[1] // 2
    down_rows = ff // shards
    down_cut = lax.dynamic_slice_in_dim(
        ffn_down.reshape(parts, ff, own), si * down_rows, down_rows, 1
    )
    down_w = (
        lax.all_gather(exchange(down_cut), "seq").transpose(0, 2, 1, 3).reshape(ff, width)
    )

    projected = product(hidden_one, attn_w)
    rounded = projected[:, : 2 * HK + HV].astype(low)
    gate_pre = projected[:, 2 * HK + HV :]
    low_rank = product(hidden_one, down_full).astype(low)
    logits = product(low_rank, decay_up) + decay_bias.astype(wide)
    log_decay = jax.nn.log_sigmoid(logits) / logit_norm

    def chunked(rows):
        return rows.reshape(parts * blocks, BLOCK, -1)

    q = chunked(rounded[:, :HK].astype(wide))
    k = chunked(rounded[:, HK : 2 * HK].astype(wide))
    v = chunked(rounded[:, 2 * HK :].astype(wide))
    place = jnp.arange(BLOCK)
    lower = place[:, None] >= place[None, :]
    ones_lower = lower.astype(wide)
    running = jnp.einsum("ts,bsk->btk", ones_lower, chunked(log_decay), precision=exact)
    total = running[:, -1]
    grown = jnp.exp(running)
    shrunk = jnp.exp(-running)
    to_end = jnp.exp(total[:, None] - running)
    qd = q * grown
    kd = k * shrunk
    kf = k * to_end
    scores = jnp.where(lower[None], fine_dot("btk,bsk->bts", qd, kd), 0.0)
    intra = fine_dot("bts,bsv->btv", scores, v)
    added = fine_dot("bsk,bsv->bkv", kf, v)
    added_c = added.reshape(parts, blocks, HK, HV)
    total_c = total.reshape(parts, blocks, HK)
    factor_c = jnp.exp(total_c)[..., None]
    local_state = added_c[:, 0]
    for c in range(1, blocks):
        local_state = factor_c[:, c] * local_state + added_c[:, c]
    totals = lax.all_gather(jnp.sum(total_c, axis=1), "seq")
    states = lax.all_gather(local_state.astype(low), "seq")
    index = jnp.arange(shards)
    upto = jnp.cumsum(totals, axis=0)
    mine_upto = lax.dynamic_index_in_dim(upto, si, 0, False)
    mine_total = lax.dynamic_index_in_dim(totals, si, 0, False)
    before = (index < si)[:, None, None]
    after = (index > si)[:, None, None]
    early = jnp.where(before, jnp.exp(jnp.where(before, mine_upto - mine_total - upto, 0.0)), 0.0)
    late = jnp.where(
        after, jnp.exp(jnp.where(after, upto - totals - mine_upto, 0.0)), 0.0
    )
    incoming = jnp.sum(early[..., None] * states.astype(wide), axis=0)
    entering = [incoming]
    for c in range(blocks):
        entering.append(factor_c[:, c] * entering[-1] + added_c[:, c])
    state_in = jnp.stack(entering[:-1], axis=1).reshape(parts * blocks, HK, HV)
    state_out = jnp.stack(entering[1:], axis=1).reshape(parts * blocks, HK, HV)
    attended = scale * (intra + fine_dot("btk,bkv->btv", qd, state_in))
    attended = attended.reshape(parts * length, HV)

    gated, gated_back = jax.vjp(gated_norm, attended, gate_pre, gain_head)
    gated_low = gated.astype(low)
    residual = x + scatter_rows(product(gated_low, out_weight))
    normed_two, norm_two_back = jax.vjp(rms_gain, residual, gain_two)
    hidden_two = gather_rows(normed_two.astype(low))
    pre = product(hidden_two, ffn_w)
    mixed, mixed_back = jax.vjp(swiglu, pre[:, :ff], pre[:, ff:])
    mixed_low = mixed.astype(low)
    d_gate_part, d_up_part = mixed_back(against(cot_low, down_w))
    d_pre = jnp.concatenate([d_gate_part.astype(low), d_up_part.astype(low)], axis=1)
    d_residual_norm, grad_ffn_gain = norm_two_back(scatter_rows(against(d_pre, ffn_w)))
    d_residual = cot_rows + d_residual_norm
    d_res_low = gather_rows(d_residual.astype(low))
    block_output = residual + scatter_rows(product(mixed_low, down_w))
    ffn_owned = owned_columns(
        jnp.concatenate(
            [transposed(hidden_two, d_pre).astype(low), transposed(cot_low, mixed_low).astype(low)],
            axis=1,
        ),
        parts,
    )

    d_attended, d_gate_pre, grad_head_gain = gated_back(against(d_res_low, out_weight))
    d_out = chunked(scale * d_attended)
    pulled = fine_dot("btk,btv->bkv", qd, d_out)
    pulled_c = pulled.reshape(parts, blocks, HK, HV)
    local_pull = pulled_c[:, blocks - 1]
    for c in range(blocks - 2, -1, -1):
        local_pull = factor_c[:, c] * local_pull + pulled_c[:, c]
    pulls = lax.all_gather(local_pull.astype(low), "seq")
    later = jnp.sum(late[..., None] * pulls.astype(wide), axis=0)
    leaving = [later]
    for c in range(blocks - 1, 0, -1):
        leaving.insert(0, factor_c[:, c] * leaving[0] + pulled_c[:, c])
    d_state = jnp.stack(leaving, axis=1).reshape(parts * blocks, HK, HV)
    d_scores = jnp.where(lower[None], fine_dot("btv,bsv->bts", d_out, v), 0.0)
    d_q = grown * (
        fine_dot("bts,bsk->btk", d_scores, kd) + fine_dot("btv,bkv->btk", d_out, state_in)
    )
    d_k = shrunk * fine_dot("bts,btk->bsk", d_scores, qd) + to_end * fine_dot(
        "bsv,bkv->bsk", v, d_state
    )
    d_v = fine_dot("bts,btv->bsv", scores, d_out) + fine_dot("bsk,bkv->bsv", kf, d_state)
    tail_term = jnp.sum(d_state * state_out, axis=2)
    d_log_decay = (
        jnp.einsum("st,bsk->btk", ones_lower, q * d_q - k * d_k, precision=exact)
        + tail_term[:, None]
    )
    d_logits = d_log_decay.reshape(parts * length, HK) * jax.nn.sigmoid(-logits) / logit_norm
    grad_decay_bias = jnp.sum(d_logits, axis=0)
    d_logits_low = d_logits.astype(low)
    grad_decay_up = transposed(low_rank, d_logits_low)
    d_low_rank = against(d_logits_low, decay_up).astype(low)
    grad_decay_down = transposed(hidden_one, d_low_rank)
    d_projected = jnp.concatenate(
        [
            d_q.reshape(parts * length, HK).astype(low),
            d_k.reshape(parts * length, HK).astype(low),
            d_v.reshape(parts * length, HV).astype(low),
            d_gate_pre.astype(low),
        ],
        axis=1,
    )
    d_hidden_one = scatter_rows(against(d_projected, attn_w) + against(d_low_rank, down_full))
    d_input_norm, grad_attn_gain = norm_one_back(d_hidden_one)
    input_grad = d_residual + d_input_norm
    attn_owned = owned_columns(transposed(hidden_one, d_projected), parts)

    devices = shards * parts
    turned = [(s * parts + f, f * shards + s) for s in range(shards) for f in range(parts)]
    out_part = lax.psum_scatter(
        transposed(gated_low, d_res_low).astype(low), "seq", scatter_dimension=0, tiled=True
    )
    own_out = lax.ppermute(out_part, ("seq", "fsdp"), turned).astype(wide)
    head_part = lax.psum_scatter(
        jnp.concatenate(
            [
                grad_decay_up.reshape(rank, shards, -1).transpose(1, 0, 2).reshape(shards, -1),
                grad_decay_bias.reshape(shards, -1),
            ],
            axis=1,
        ),
        "seq",
        scatter_dimension=0,
        tiled=True,
    )
    head_part = lax.ppermute(head_part, ("seq", "fsdp"), turned)[0]
    own_bias_size = HK // shards
    own_up = head_part[: rank * own_bias_size].reshape(rank, own_bias_size)
    own_bias = head_part[rank * own_bias_size :]
    summed = jnp.concatenate(
        [
            grad_attn_gain.reshape(devices, -1),
            grad_ffn_gain.reshape(devices, -1),
            grad_head_gain.reshape(devices, -1),
            grad_decay_down.reshape(devices, -1),
        ],
        axis=1,
    )
    summed = lax.psum_scatter(summed, "seq", scatter_dimension=0, tiled=True)
    summed = lax.psum_scatter(summed, "fsdp", scatter_dimension=0, tiled=True)[0]
    each = width // devices
    each_head = HV // devices
    own_attn_gain = summed[:each]
    own_ffn_gain = summed[each : 2 * each]
    own_head_gain = summed[2 * each : 2 * each + each_head]
    own_down = summed[2 * each + each_head :].reshape(each, rank)
    return (
        block_output[None],
        input_grad[None],
        own_attn_gain,
        across(attn_owned[:, :, :HK]),
        across(attn_owned[:, :, HK : 2 * HK]),
        across(attn_owned[:, :, 2 * HK : 2 * HK + HV]),
        across(attn_owned[:, :, 2 * HK + HV :]),
        own_down,
        own_up,
        own_bias,
        own_head_gain,
        own_out,
        own_ffn_gain,
        across(ffn_owned[:, :, :ff]),
        across(ffn_owned[:, :, ff : 2 * ff]),
        across(ffn_owned[:, :, 2 * ff :]).T,
    )


def solution(mesh):
    return jax.shard_map(
        on_device,
        mesh=mesh,
        in_specs=(
            P("fsdp", "seq", None),
            P("fsdp"),
            P("fsdp", None),
            P("fsdp", None),
            P("fsdp", None),
            P("fsdp", None),
            P("fsdp", None),
            P(None, "fsdp"),
            P("fsdp"),
            P("fsdp"),
            P("fsdp", None),
            P("fsdp"),
            P("fsdp", None),
            P("fsdp", None),
            P(None, "fsdp"),
            P("fsdp", "seq", None),
        ),
        out_specs=(
            P("fsdp", "seq", None),
            P("fsdp", "seq", None),
            P(("seq", "fsdp")),
            P(("seq", "fsdp"), None),
            P(("seq", "fsdp"), None),
            P(("seq", "fsdp"), None),
            P(("seq", "fsdp"), None),
            P(("seq", "fsdp"), None),
            P(None, ("seq", "fsdp")),
            P(("seq", "fsdp")),
            P(("seq", "fsdp")),
            P(("seq", "fsdp"), None),
            P(("seq", "fsdp")),
            P(("seq", "fsdp"), None),
            P(("seq", "fsdp"), None),
            P(None, ("seq", "fsdp")),
        ),
        check_vma=False,
    )
```

time: 1470 us -> 668 us (0.45)
  waiting for transfers between devices: 1100 us -> 388 us
  matrix products: 103 us -> 48.6 us
  other arithmetic: 62.5 us -> 30.3 us
    reduce_scatter x16 -> x7, waiting for transfers between devices: 651 us -> 153 us  [the longest x2 81.2 us: owned_columns(): lax.psum_scatter(grads.astype(low), 'seq', scatter_dimension=0, tiled=True)]
    all_gather x10 -> x9, waiting for transfers between devices: 417 us -> 186 us  [the longest x4 89.4 us: gather_rows(): return lax.all_gather(rows, 'fsdp', axis=0, tiled=True)]
    all_gather x7 -> x1, blocking collectives: 73.2 us -> 8.87 us  [on_device(): totals = lax.all_gather(jnp.sum(total_c, axis=1), 'seq')]
    dot_general x58 -> x32, matrix products: 102 us -> 48.6 us  [the longest x6 15.1 us: product(): return jnp.dot(left, right, preferred_element_type=wide)]
    all_to_all x0 -> x3, blocking collectives: none -> 48.7 us  [exchange(): return lax.all_to_all(pieces, 'fsdp', 0, 0)]
    unnamed x3, blocking collectives: 45 us -> 67.8 us
    unnamed x34 -> x18, waiting for transfers between devices: 27.6 us -> 49.8 us
    convert_element_type x38 -> x10, other arithmetic: 30.6 us -> 9.84 us  [the longest x1 1.86 us: on_device(): hidden_one = gather_rows(normed_one.astype(low))]
  transfers between devices with their start and end apart: 30 -> 21, of which waited for: 25 -> 15; matrix products, arithmetic and copies ran while one was open for 11% -> 11% of each run, Pallas kernels for 0% -> 0%
where the time goes in v1:
time: 668 us; the launch traced here: 666 us
  waiting for transfers between devices  388 us (58%)
  blocking collectives  125 us (19%)
  matrix products  48.6 us (7%)
  local copies, waits for them, and re-layouts  44.6 us (7%)
  other arithmetic  30.3 us (5%)
  between operations  16.4 us (2%)
  starting transfers between devices  12.5 us (2%)
    all_gather x4, waiting for transfers between devices, gather_rows(): return lax.all_gather(rows, 'fsdp', axis=0, tiled=True)  89.4 us
    reduce_scatter x2, waiting for transfers between devices, owned_columns(): lax.psum_scatter(grads.astype(low), 'seq', scatter_dimension=0, tiled=True)  81.2 us
    unnamed x3, blocking collectives  67.8 us
    all_gather x2, waiting for transfers between devices, column_owned(): got = lax.all_gather(exchange(sent), 'seq')  52.8 us
    unnamed x18, waiting for transfers between devices  49.8 us
    all_to_all x3, blocking collectives, exchange(): return lax.all_to_all(pieces, 'fsdp', 0, 0)  48.7 us
    reduce_scatter x4, waiting for transfers between devices, scatter_rows(): lax.psum_scatter(rows.astype(low), 'fsdp', scatter_dimension=0, tiled=True)  41.6 us
    reduce_scatter x1, waiting for transfers between devices, on_device(): lax.psum_scatter(transposed(gated_low, d_res_low).astype(low), 'seq', sca...  30.3 us
  transfers between devices with their start and end apart: 21, of which 15 were waited for; matrix products, arithmetic and copies ran while one was open for 11% of the time, Pallas kernels for 0%

profile of v1, /device:TPU:0, one launch (start us, length us, event | category | flops | bytes accessed | tf_op | source)
XLA Modules:
  0.0 666.4 jit_solution(6801367049386223646)
XLA Ops:
  10.3 2.1 concatenate.24
  12.8 21.1 %all-reduce = bf16[18688]{0:T(1024)(128)(2,1)S(1)} all-reduce(bf16[18688]{0:T(1024)(128)(2,1)S(1)} %dynamic-update-slice), channel_id=2, replica_groups=mesh['seq'=8,'fsdp'=4] {'fsdp'}, use_global_device_ids=true, to_apply=%add | all-reduce | flops 18688 | bytes 74752
  35.9 1.9 multiply_convert_fusion.3
  39.8 14.0 %all_to_all.25 = bf16[4,32,768]{2,1,0:T(8,128)(2,1)} all-to-all(bf16[4,32,768]{2,1,0:T(8,128)(2,1)S(1)} %copy.196), channel_id=1, replica_groups=mesh['seq'=8,'fsdp'=4] {'fsdp'}, dimensions={0} | all-to-all | bytes 393216 | tf_op jit(solution)/shard_map/all_to_all | solution.py:52
  54.2 12.5 %all-gather.16.cloned.1.call-done = bf16[512,1024]{1,0:T(8,128)(2,1)} async-done(((bf16[128,1024]{1,0:T(8,128)(2,1)}), bf16[512,1024]{1,0:T(8,128)(2,1)}) %all-gather.16.cloned.1.call-update) | async-done | bytes 1048592 | tf_op jit(solution)/shard_map/all_gather | solution.py:56
  69.7 23.4 %all-gather.28.cloned.1.call-done = bf16[32,32,768]{2,1,0:T(8,128)(2,1)} async-done(((bf16[4,32,768]{2,1,0:T(8,128)(2,1)}), bf16[32,32,768]{2,1,0:T(8,128)(2,1)}) %all-gather.28.cloned.1.call-update) | async-done | bytes 1572880 | tf_op jit(solution)/shard_map/all_gather | solution.py:69
  93.1 1.6 copy.197
  94.8 2.2 fusion.66
  99.3 8.9 %all-gather.5 = f32[8,4,128]{2,1,0:T(4,128)S(1)} all-gather(f32[1,4,128]{2,1,0:T(4,128)S(1)} %bitcast.327), channel_id=4, replica_groups=mesh['seq'=8,'fsdp'=4] {'seq'}, dimensions={0}, use_global_device_ids=true | all-gather | bytes 18432 | tf_op jit(solution)/shard_map/all_gather | solution.py:170
  111.1 15.4 %all-gather.18.cloned.1.call-done = bf16[8,4,128,256]{3,2,1,0:T(8,128)(2,1)} async-done(((bf16[1,4,128,256]{3,2,1,0:T(8,128)(2,1)}), bf16[8,4,128,256]{3,2,1,0:T(8,128)(2,1)}) %all-gather.18.cloned.1.call-update) | async-done | bytes 2097168 | tf_op jit(solution)/shard_map/all_gather | solution.py:171
  126.4 2.0 multiply_reduce_fusion.1
  135.4 16.1 %all_to_all.26 = bf16[4,88,256]{2,1,0:T(8,128)(2,1)} all-to-all(bf16[4,88,256]{2,1,0:T(8,128)(2,1)S(1)} %constant_dynamic-slice_fusion), channel_id=1, replica_groups=mesh['seq'=8,'fsdp'=4] {'fsdp'}, dimensions={0} | all-to-all | bytes 360448 | tf_op jit(solution)/shard_map/all_to_all | solution.py:52
  153.4 18.6 %all_to_all.27 = bf16[4,32,1408]{2,1,0:T(8,128)(2,1)} all-to-all(bf16[4,32,1408]{2,1,0:T(8,128)(2,1)S(1)} %copy.202), channel_id=1, replica_groups=mesh['seq'=8,'fsdp'=4] {'fsdp'}, dimensions={0} | all-to-all | bytes 720896 | tf_op jit(solution)/shard_map/all_to_all | solution.py:52
  173.3 1.8 multiply_convert_fusion.1
  176.1 19.9 %all-gather.32.cloned.1.call-done = bf16[32,88,256]{2,1,0:T(8,128)(2,1)} async-done(((bf16[4,88,256]{2,1,0:T(8,128)(2,1)}), bf16[32,88,256]{2,1,0:T(8,128)(2,1)}) %all-gather.32.cloned.1.call-update) | async-done | bytes 1441808 | tf_op jit(solution)/shard_map/all_gather | solution.py:134
  196.1 2.0 copy.204
  199.5 29.4 %all-gather.30.cloned.1.call-done = bf16[32,32,1408]{2,1,0:T(8,128)(2,1)} async-done(((bf16[4,32,1408]{2,1,0:T(8,128)(2,1)}), bf16[32,32,1408]{2,1,0:T(8,128)(2,1)}) %all-gather.30.cloned.1.call-update) | async-done | bytes 2883600 | tf_op jit(solution)/shard_map/all_gather | solution.py:69
  228.9 3.7 copy.203
  232.6 26.5 %all-gather.20.cloned.1.call-done = bf16[512,1024]{1,0:T(8,128)(2,1)} async-done(((bf16[128,1024]{1,0:T(8,128)(2,1)}), bf16[512,1024]{1,0:T(8,128)(2,1)}) %all-gather.20.cloned.1.call-update) | async-done | bytes 1048592 | tf_op jit(solution)/shard_map/all_gather | solution.py:56
  259.1 5.6 fusion.71
  264.7 23.9 %all-gather.22.cloned.1.call-done = bf16[512,1024]{1,0:T(8,128)(2,1)} async-done(((bf16[128,1024]{1,0:T(8,128)(2,1)}), bf16[512,1024]{1,0:T(8,128)(2,1)}) %all-gather.22.cloned.1.call-update) | async-done | bytes 1048592 | tf_op jit(solution)/shard_map/all_gather | solution.py:56
  288.6 4.6 fusion.2
  294.4 2.8 convolution_convert_fusion.3
  297.4 26.7 %reduce-scatter.12.cloned.1.call-done = bf16[128,1024]{1,0:T(8,128)(2,1)} async-done(((bf16[512,1024]{1,0:T(8,128)(2,1)}), bf16[128,1024]{1,0:T(8,128)(2,1)}) %reduce-scatter.12.cloned.1.call-update) | async-done | bytes 262160 | tf_op jit(solution)/shard_map/reduce_scatter | solution.py:60
  324.1 1.8 fusion.17
  325.9 1.8 fusion.60
  327.9 26.6 %all-gather.24.cloned.1.call-done = bf16[512,1024]{1,0:T(8,128)(2,1)} async-done(((bf16[128,1024]{1,0:T(8,128)(2,1)}), bf16[512,1024]{1,0:T(8,128)(2,1)}) %all-gather.24.cloned.1.call-update) | async-done | bytes 1048592 | tf_op jit(solution)/shard_map/all_gather | solution.py:56
  354.4 2.7 multiply_reduce_fusion.2
  357.2 2.2 fusion.20
  361.9 3.3 fusion.5
  365.2 2.7 copy.218
  367.9 3.5 convolution_convert_fusion
  371.4 2.4 pad_maximum_fusion
  378.6 2.4 fusion.68
  381.0 8.1 %all-gather.26.cloned.1.call-done = bf16[8,4,128,256]{3,2,1,0:T(8,128)(2,1)} async-done(((bf16[1,4,128,256]{3,2,1,0:T(8,128)(2,1)}), bf16[8,4,128,256]{3,2,1,0:T(8,128)(2,1)}) %all-gather.26.cloned.1.call-update) | async-done | bytes 2097168 | tf_op jit(solution)/shard_map/all_gather | solution.py:220
  389.1 2.1 multiply_reduce_fusion
  398.3 3.1 convolution_convert_fusion.4
  401.4 43.6 %reduce-scatter.20.cloned.1.call-done = bf16[128,2112]{1,0:T(8,128)(2,1)} async-done(((bf16[1024,2112]{1,0:T(8,128)(2,1)}), bf16[128,2112]{1,0:T(8,128)(2,1)}) %reduce-scatter.20.cloned.1.call-update) | async-done | bytes 540688 | tf_op jit(solution)/shard_map/reduce_scatter | solution.py:74
  445.0 4.6 all-to-all-start.4
  449.6 2.2 convolution_convert_fusion.1
  451.9 30.3 %reduce-scatter.18.cloned.1.call-done = bf16[32,1024]{1,0:T(8,128)(2,1)} async-done(((bf16[256,1024]{1,0:T(8,128)(2,1)}), bf16[32,1024]{1,0:T(8,128)(2,1)}) %reduce-scatter.18.cloned.1.call-update) | async-done | bytes 65552 | tf_op jit(solution)/shard_map/reduce_scatter | solution.py:261
  491.4 28.0 %all-reduce.3 = f32[8,272]{1,0:T(8,128)S(1)} all-reduce(f32[8,272]{1,0:T(8,128)S(1)} %pad_maximum_fusion.10), channel_id=14, replica_groups=mesh['seq'=8,'fsdp'=4] {'seq'}, use_global_device_ids=true, to_apply=%region_22.23.clone | all-reduce | flops 2176 | bytes 17408
  524.9 14.8 %reduce-scatter.10.cloned.1.call-done = bf16[128,1024]{1,0:T(8,128)(2,1)} async-done(((bf16[512,1024]{1,0:T(8,128)(2,1)}), bf16[128,1024]{1,0:T(8,128)(2,1)}) %reduce-scatter.10.cloned.1.call-update) | async-done | bytes 262160 | tf_op jit(solution)/shard_map/reduce_scatter | solution.py:60
  539.7 2.5 fusion.25
  542.2 37.6 %reduce-scatter.16.cloned.1.call-done = bf16[128,768]{1,0:T(8,128)(2,1)} async-done(((bf16[1024,768]{1,0:T(8,128)(2,1)}), bf16[128,768]{1,0:T(8,128)(2,1)}) %reduce-scatter.16.cloned.1.call-update) | async-done | bytes 196624 | tf_op jit(solution)/shard_map/reduce_scatter | solution.py:74
  579.7 4.6 all-to-all-start.3
  584.3 49.5 %all-reduce.6.cloned.1.call-done = f32[32,584]{1,0:T(8,128)} async-done(((f32[32,584]{1,0:T(8,128)}), f32[32,584]{1,0:T(8,128)}) %all-reduce.6.cloned.1.call-update) | async-done | bytes 74768
  634.6 18.7 %all-reduce.2 = f32[4,584]{1,0:T(4,128)S(1)} all-reduce(f32[4,584]{1,0:T(4,128)S(1)} %constant_dynamic-slice_fusion.11), channel_id=12, replica_groups=mesh['seq'=8,'fsdp'=4] {'fsdp'}, use_global_device_ids=true, to_apply=%region_19.20.clone | all-reduce | flops 2336 | bytes 18688
  (340 shorter events, 64.3 us)
Async XLA Ops:
  7.2 128.2 %copy-start = (bf16[2816,256]{1,0:T(8,128)(2,1)S(1)}, bf16[2816,256]{1,0:T(8,128)(2,1)}, u32[]{:S(2)}) copy-start(bf16[2816,256]{1,0:T(8,128)(2,1)} %param.30) | copy-start | bytes 4325380
  7.2 59.5 %all-gather.16.cloned.1.call-start = ((), (), s32[]{:S(2)}) async-start(), calls=%async_computation.12 | async-start | bytes 1310720 | tf_op jit(solution)/shard_map/all_gather | solution.py:56
  37.7 55.3 %all-gather.28.cloned.1.call-start = ((), (), s32[]{:S(2)}) async-start(), calls=%async_computation.25 | async-start | bytes 1769472 | tf_op jit(solution)/shard_map/all_gather | solution.py:69
  39.6 28.7 %copy-start.75 = (bf16[16,128]{1,0:T(8,128)(2,1)S(1)}, bf16[16,128]{1,0:T(8,128)(2,1)}, u32[]{:S(2)}) copy-start(bf16[16,128]{1,0:T(8,128)(2,1)} %param.23) | copy-start | bytes 12292
  53.8 72.6 %all-gather.18.cloned.1.call-start = ((), (), s32[]{:S(2)}) async-start(), calls=%async_computation.13 | async-start | bytes 2359296 | tf_op jit(solution)/shard_map/all_gather | solution.py:171
  54.2 40.5 %copy-start.31 = (bf16[1024,16]{1,0:T(8,128)(2,1)}, bf16[1024,16]{1,0:T(8,128)(2,1)S(1)}, u32[]{:S(2)}) copy-start(bf16[1024,16]{1,0:T(8,128)(2,1)S(1)} %reshape.381) | copy-start | bytes 98308
  69.7 58.7 %copy-start.59 = (f32[4,1,128,1]{2,1,0,3:T(1,128)}, f32[4,1,128,1]{2,1,0,3:T(1,128)S(1)}, u32[]{:S(2)}) copy-start(f32[4,1,128,1]{2,1,0,3:T(1,128)S(1)} %get-tuple-element.167) | copy-start | bytes 6148
  69.7 58.7 %copy-start.61 = (f32[4,1,128,1]{2,1,0,3:T(1,128)}, f32[4,1,128,1]{2,1,0,3:T(1,128)S(1)}, u32[]{:S(2)}) copy-start(f32[4,1,128,1]{2,1,0,3:T(1,128)S(1)} %get-tuple-element.166) | copy-start | bytes 6148
  97.1 33.1 %copy-start.18 = (bf16[512,128]{1,0:T(8,128)(2,1)}, bf16[512,128]{1,0:T(8,128)(2,1)S(1)}, u32[]{:S(2)}) copy-start(bf16[512,128]{1,0:T(8,128)(2,1)S(1)} %get-tuple-element.147) | copy-start | bytes 393220
  98.5 73.7 %reduce-scatter.8.cloned.1.call-start = ((), (), s32[]{:S(2)}) async-start(), calls=%async_computation.14 | async-start | bytes 1310720 | tf_op jit(solution)/shard_map/reduce_scatter | solution.py:60
  135.3 60.7 %all-gather.32.cloned.1.call-start = ((), (), s32[]{:S(2)}) async-start(), calls=%async_computation.27 | async-start | bytes 1622016 | tf_op jit(solution)/shard_map/all_gather | solution.py:134
  151.5 77.4 %all-gather.30.cloned.1.call-start = ((), (), s32[]{:S(2)}) async-start(), calls=%async_computation.26 | async-start | bytes 3244032 | tf_op jit(solution)/shard_map/all_gather | solution.py:69
  172.0 87.0 %all-gather.20.cloned.1.call-start = ((), (), s32[]{:S(2)}) async-start(), calls=%async_computation.15 | async-start | bytes 1310720 | tf_op jit(solution)/shard_map/all_gather | solution.py:56
  172.1 153.8 %copy-start.52 = (f32[1,2,4,128]{3,1,2,0:T(2,128)}, f32[1,2,4,128]{3,1,2,0:T(2,128)S(1)}, u32[]{:S(2)}) copy-start(f32[1,2,4,128]{3,1,2,0:T(2,128)S(1)} %copy.238) | copy-start | bytes 12292
  175.1 113.5 %all-gather.22.cloned.1.call-start = ((), (), s32[]{:S(2)}) async-start(), calls=%async_computation.17 | async-start | bytes 1310720 | tf_op jit(solution)/shard_map/all_gather | solution.py:56
  175.9 148.2 %reduce-scatter.12.cloned.1.call-start = ((), (), s32[]{:S(2)}) async-start(), calls=%async_computation.18 | async-start | bytes 1310720 | tf_op jit(solution)/shard_map/reduce_scatter | solution.py:60
  259.1 29.5 %copy-start.38 = (bf16[88,8,4,256]{3,1,2,0:T(8,128)(2,1)S(1)}, bf16[88,8,4,256]{3,1,2,0:T(8,128)(2,1)}, u32[]{:S(2)}) copy-start(bf16[88,8,4,256]{3,1,2,0:T(8,128)(2,1)} %copy.239) | copy-start | bytes 4325380
  294.4 29.7 %copy-start.5 = (bf16[128,1024]{1,0:T(8,128)(2,1)S(1)}, bf16[128,1024]{1,0:T(8,128)(2,1)}, u32[]{:S(2)}) copy-start(bf16[128,1024]{1,0:T(8,128)(2,1)} %reduce-scatter.8.cloned.1.call-done) | copy-start | bytes 786436
  294.4 29.7 %copy-start.72 = (f32[128]{0:T(128)S(1)}, f32[128]{0:T(128)}, u32[]{:S(2)}) copy-start(f32[128]{0:T(128)} %copy-done.71) | copy-start | bytes 1540
  297.3 28.6 %copy-start.10 = (f32[1,128,1024]{2,1,0:T(8,128)S(1)}, f32[1,128,1024]{2,1,0:T(8,128)}, u32[]{:S(2)}) copy-start(f32[1,128,1024]{2,1,0:T(8,128)} %param.31) | copy-start | bytes 1572868
  297.3 57.1 %copy-start.13 = (f32[8,64,256]{2,1,0:T(8,128)S(1)}, f32[8,64,256]{2,1,0:T(8,128)}, u32[]{:S(2)}) copy-start(f32[8,64,256]{2,1,0:T(8,128)} %copy-done.12) | copy-start | bytes 1572868
  297.3 57.1 %copy-start.66 = (f32[512]{0:T(512)S(1)}, f32[512]{0:T(512)}, u32[]{:S(2)}) copy-start(f32[512]{0:T(512)} %copy-done.65) | copy-start | bytes 6148
  297.3 57.1 %copy-start.70 = (f32[256]{0:T(256)S(1)}, f32[256]{0:T(256)}, u32[]{:S(2)}) copy-start(f32[256]{0:T(256)} %reshape.414) | copy-start | bytes 3076
  297.4 57.1 %all-gather.24.cloned.1.call-start = ((), (), s32[]{:S(2)}) async-start(), calls=%async_computation.19 | async-start | bytes 1310720 | tf_op jit(solution)/shard_map/all_gather | solution.py:56
  325.9 31.2 %copy-start.77 = (f32[128]{0:T(128)}, f32[128]{0:T(128)S(1)}, u32[]{:S(2)}) copy-start(f32[128]{0:T(128)S(1)} %multiply_multiply_fusion.2) | copy-start | bytes 1540
  327.8 29.3 %copy-start.64 = (f32[512]{0:T(512)S(1)}, f32[512]{0:T(512)}, u32[]{:S(2)}) copy-start(f32[512]{0:T(512)} %copy-done.63) | copy-start | bytes 6148
  327.8 61.3 %all-gather.26.cloned.1.call-start = ((), (), s32[]{:S(2)}) async-start(), calls=%async_computation.20 | async-start | bytes 2359296 | tf_op jit(solution)/shard_map/all_gather | solution.py:220
  361.8 83.2 %reduce-scatter.20.cloned.1.call-start = ((), (), s32[]{:S(2)}) async-start(), calls=%async_computation.24 | async-start | bytes 5013504 | tf_op jit(solution)/shard_map/reduce_scatter | solution.py:74
  373.8 108.4 %reduce-scatter.18.cloned.1.call-start = ((), (), s32[]{:S(2)}) async-start(), calls=%async_computation.23 | async-start | bytes 589824 | tf_op jit(solution)/shard_map/reduce_scatter | solution.py:261
  381.0 141.9 %reduce-scatter.14.cloned.1.call-start = ((), (), s32[]{:S(2)}) async-start(), calls=%async_computation.21 | async-start | bytes 1310720 | tf_op jit(solution)/shard_map/reduce_scatter | solution.py:60
  398.1 141.6 %reduce-scatter.10.cloned.1.call-start = ((), (), s32[]{:S(2)}) async-start(), calls=%async_computation.16 | async-start | bytes 1310720 | tf_op jit(solution)/shard_map/reduce_scatter | solution.py:60
  401.4 48.2 %copy-start.22 = (bf16[512,1024]{1,0:T(8,128)(2,1)S(1)}, bf16[512,1024]{1,0:T(8,128)(2,1)}, u32[]{:S(2)}) copy-start(bf16[512,1024]{1,0:T(8,128)(2,1)} %all-gather.16.cloned.1.call-done) | copy-start | bytes 3145732
  401.4 48.2 %copy-start.47 = (bf16[8,64,256]{2,1,0:T(8,128)(2,1)S(1)}, bf16[8,64,256]{2,1,0:T(8,128)(2,1)}, u32[]{:S(2)}) copy-start(bf16[8,64,256]{2,1,0:T(8,128)(2,1)} %copy-done.46) | copy-start | bytes 786436
  401.4 48.2 %copy-start.51 = (bf16[8,64,128]{2,1,0:T(8,128)(2,1)S(1)}, bf16[8,64,128]{2,1,0:T(8,128)(2,1)}, u32[]{:S(2)}) copy-start(bf16[8,64,128]{2,1,0:T(8,128)(2,1)} %copy-done.50) | copy-start | bytes 393220
  445.0 42.0 %all-to-all-start.4 = ((bf16[4,32,2112]{2,1,0:T(8,128)(2,1)}), bf16[4,32,2112]{2,1,0:T(8,128)(2,1)S(1)}, u32[]{:S(2)}, u32[]{:S(2)}) async-start(bf16[4,32,2112]{2,1,0:T(8,128)(2,1)} %bitcast.294), calls=%async_computation.11 | async-start | bytes 1114112 | tf_op jit(solution)/shard_map/all_to_all | solution.py:52
  449.6 130.1 %reduce-scatter.16.cloned.1.call-start = ((), (), s32[]{:S(2)}) async-start(), calls=%async_computation.22 | async-start | bytes 1769472 | tf_op jit(solution)/shard_map/reduce_scatter | solution.py:74
  451.8 31.9 %copy-start.84 = (u32[32]{0:T(128)S(1)}, u32[32]{0:T(128)}, u32[]{:S(2)}) copy-start(u32[32]{0:T(128)} %constant.70) | copy-start | bytes 388
  451.8 33.1 %copy-start.67 = (f32[1024]{0:T(1024)S(1)}, f32[1024]{0:T(1024)}, u32[]{:S(2)}) copy-start(f32[1024]{0:T(1024)} %get-tuple-element.130) | copy-start | bytes 12292
  451.8 33.8 %copy-start.78 = (f32[256]{0:T(256)S(1)}, f32[256]{0:T(256)}, u32[]{:S(2)}) copy-start(f32[256]{0:T(256)} %get-tuple-element.128) | copy-start | bytes 3076
  451.9 182.0 %all-reduce.6.cloned.1.call-start = ((), (), s32[]{:S(2)}) async-start(), calls=%async_computation.28 | async-start | bytes 163840
  482.2 4.1 collective-permute-start.1
  489.9 32.9 %copy-start.54 = (f32[1,2,4,128]{3,1,2,0:T(2,128)S(1)}, f32[1,2,4,128]{3,1,2,0:T(2,128)}, u32[]{:S(2)}) copy-start(f32[1,2,4,128]{3,1,2,0:T(2,128)} %copy-done.53) | copy-start | bytes 12292
  489.9 32.9 %copy-start.74 = (f32[128]{0:T(128)S(1)}, f32[128]{0:T(128)}, u32[]{:S(2)}) copy-start(f32[128]{0:T(128)} %copy-done.73) | copy-start | bytes 1540
  491.3 32.8 %copy-start.55 = (f32[32,32]{1,0:T(8,128)S(1)}, f32[32,32]{1,0:T(8,128)}, u32[]{:S(2)}) copy-start(f32[32,32]{1,0:T(8,128)} %reshape.399) | copy-start | bytes 12292
  491.3 32.8 %copy-start.56 = (f32[32,8]{1,0:T(8,128)S(1)}, f32[32,8]{1,0:T(8,128)}, u32[]{:S(2)}) copy-start(f32[32,8]{1,0:T(8,128)} %reshape.400) | copy-start | bytes 3076
  520.1 1.6 collective-permute-start
  539.7 120.1 %copy-start.1 = (bf16[2816,256]{1,0:T(8,128)(2,1)S(1)}, bf16[2816,256]{1,0:T(8,128)(2,1)}, u32[]{:S(2)}) copy-start(bf16[2816,256]{1,0:T(8,128)(2,1)} %param.30) | copy-start | bytes 4325380
  579.7 77.4 %all-to-all-start.3 = ((bf16[4,32,768]{2,1,0:T(8,128)(2,1)}), bf16[4,32,768]{2,1,0:T(8,128)(2,1)S(1)}, u32[]{:S(2)}, u32[]{:S(2)}) async-start(bf16[4,32,768]{2,1,0:T(8,128)(2,1)} %bitcast.300), calls=%async_computation.8 | async-start | bytes 393216 | tf_op jit(solution)/shard_map/all_to_all | solution.py:52
  (62 other events, 333.1 us)
Sparse Core Ops, SparseCore 0:
  37.9 28.7 all-gather.15
  68.6 24.4 all-gather.27
  98.6 27.7 all-gather.17
  135.5 31.8 reduce-scatter.7
  169.1 26.8 all-gather.31
  197.8 31.0 all-gather.29
  231.0 27.9 all-gather.19
  261.2 27.3 all-gather.21
  297.4 26.6 reduce-scatter.11
  327.9 26.4 all-gather.23
  361.9 27.1 all-gather.25
  392.4 52.5 reduce-scatter.19
  448.1 34.0 reduce-scatter.17
  484.4 27.2 reduce-scatter.13
  513.8 25.8 reduce-scatter.9
  542.9 36.8 reduce-scatter.15
  583.2 50.5 all-reduce.5

commit v2 on v1

--- a/solution.py
+++ b/solution.py
@@ -60,20 +60,12 @@
     return lax.psum_scatter(rows.astype(low), "fsdp", scatter_dimension=0, tiled=True).astype(wide)
 
 
-def column_owned(weights, parts, si, shards):
-    rows = weights[0].shape[0] // shards
-    cuts = [
-        lax.dynamic_slice_in_dim(w, si * rows, rows, 0).reshape(rows, parts, -1) for w in weights
-    ]
-    sent = jnp.concatenate(cuts, axis=2).transpose(1, 0, 2)
-    got = lax.all_gather(exchange(sent), "seq")
-    return got.transpose(1, 0, 2, 3).reshape(parts * shards * rows, -1)
-
-
-def owned_columns(grads, parts):
-    section = lax.psum_scatter(grads.astype(low), "seq", scatter_dimension=0, tiled=True)
-    rows = section.shape[0] // parts
-    return exchange(section.reshape(parts, rows, -1))
+def summed_rows(grads):
+    return lax.psum_scatter(grads.astype(low), "seq", scatter_dimension=0, tiled=True)
+
+
+def owned_columns(section, parts):
+    return exchange(section.reshape(parts, section.shape[0] // parts, -1))
 
 
 def across(pieces):
@@ -107,9 +99,8 @@
     blocks = length // BLOCK
     scale = HK ** (-0.5)
 
-    small = lax.all_gather(
-        jnp.concatenate([attn_gain, ffn_gain, head_gain, decay_down.reshape(-1)]), "fsdp"
-    )
+    small = jnp.concatenate([attn_gain, ffn_gain, head_gain, decay_down.reshape(-1)])
+    small = exchange(jnp.broadcast_to(small[None], (parts, small.shape[0])))
     own = attn_gain.shape[0]
     own_head = head_gain.shape[0]
     gain_one = small[:, :own].reshape(-1).astype(wide)
@@ -119,19 +110,32 @@
     rank = down_full.shape[1]
 
     normed_one, norm_one_back = jax.vjp(rms_gain, x, gain_one)
-    hidden_one = gather_rows(normed_one.astype(low))
-    attn_w = column_owned(
-        (query_weight, key_weight, value_weight, gate_weight), parts, si, shards
-    )
-    cot_low = gather_rows(cot_rows.astype(low))
-    ffn_w = column_owned((ffn_gate, ffn_up), parts, si, shards)
-    ff = ffn_w.shape[1] // 2
+    both = gather_rows(jnp.concatenate([normed_one.astype(low), cot_rows.astype(low)], axis=1))
+    hidden_one = both[:, :width]
+    cot_low = both[:, width:]
+    ff = ffn_gate.shape[1] // parts
+    rows = own // shards
     down_rows = ff // shards
-    down_cut = lax.dynamic_slice_in_dim(
-        ffn_down.reshape(parts, ff, own), si * down_rows, down_rows, 1
+    cuts = [
+        lax.dynamic_slice_in_dim(w, si * rows, rows, 0).reshape(rows, parts, -1).transpose(1, 0, 2)
+        for w in (query_weight, key_weight, value_weight, gate_weight, ffn_gate, ffn_up)
+    ]
+    cuts.append(
+        lax.dynamic_slice_in_dim(
+            ffn_down.reshape(parts, ff, own), si * down_rows, down_rows, 1
+        ).reshape(parts, rows, -1)
+    )
+    got = lax.all_gather(exchange(jnp.concatenate(cuts, axis=2)), "seq")
+    attn_columns = 2 * HK + 2 * HV
+    attn_w = got[..., :attn_columns].transpose(1, 0, 2, 3).reshape(width, -1)
+    ffn_w = (
+        got[..., attn_columns : attn_columns + 2 * ff].transpose(1, 0, 2, 3).reshape(width, -1)
     )
     down_w = (
-        lax.all_gather(exchange(down_cut), "seq").transpose(0, 2, 1, 3).reshape(ff, width)
+        got[..., attn_columns + 2 * ff :]
+        .reshape(shards, parts, down_rows, own)
+        .transpose(0, 2, 1, 3)
+        .reshape(ff, width)
     )
 
     projected = product(hidden_one, attn_w)
@@ -198,17 +202,22 @@
     mixed_low = mixed.astype(low)
     d_gate_part, d_up_part = mixed_back(against(cot_low, down_w))
     d_pre = jnp.concatenate([d_gate_part.astype(low), d_up_part.astype(low)], axis=1)
-    d_residual_norm, grad_ffn_gain = norm_two_back(scatter_rows(against(d_pre, ffn_w)))
+    both = scatter_rows(
+        jnp.concatenate(
+            [against(d_pre, ffn_w).astype(low), product(mixed_low, down_w).astype(low)], axis=1
+        )
+    )
+    d_residual_norm, grad_ffn_gain = norm_two_back(both[:, :width])
     d_residual = cot_rows + d_residual_norm
     d_res_low = gather_rows(d_residual.astype(low))
-    block_output = residual + scatter_rows(product(mixed_low, down_w))
-    ffn_owned = owned_columns(
+    block_output = residual + both[:, width:]
+    ffn_section = summed_rows(
         jnp.concatenate(
             [transposed(hidden_two, d_pre).astype(low), transposed(cot_low, mixed_low).astype(low)],
             axis=1,
-        ),
-        parts,
-    )
+        )
+    )
+    ffn_owned = owned_columns(ffn_section, parts)
 
     d_attended, d_gate_pre, grad_head_gain = gated_back(against(d_res_low, out_weight))
     d_out = chunked(scale * d_attended)
@@ -254,47 +263,49 @@
     d_hidden_one = scatter_rows(against(d_projected, attn_w) + against(d_low_rank, down_full))
     d_input_norm, grad_attn_gain = norm_one_back(d_hidden_one)
     input_grad = d_residual + d_input_norm
-    attn_owned = owned_columns(transposed(hidden_one, d_projected), parts)
-
     devices = shards * parts
+    grad_out = transposed(gated_low, d_res_low).astype(low)
+    attn_section = summed_rows(
+        jnp.concatenate(
+            [transposed(hidden_one, d_projected).astype(low), grad_out.reshape(width, HV)], axis=1
+        )
+    )
+    attn_owned = owned_columns(attn_section[:, :attn_columns], parts)
     turned = [(s * parts + f, f * shards + s) for s in range(shards) for f in range(parts)]
-    out_part = lax.psum_scatter(
-        transposed(gated_low, d_res_low).astype(low), "seq", scatter_dimension=0, tiled=True
-    )
-    own_out = lax.ppermute(out_part, ("seq", "fsdp"), turned).astype(wide)
-    head_part = lax.psum_scatter(
-        jnp.concatenate(
-            [
-                grad_decay_up.reshape(rank, shards, -1).transpose(1, 0, 2).reshape(shards, -1),
-                grad_decay_bias.reshape(shards, -1),
-            ],
-            axis=1,
-        ),
-        "seq",
-        scatter_dimension=0,
-        tiled=True,
-    )
-    head_part = lax.ppermute(head_part, ("seq", "fsdp"), turned)[0]
+    own_out = lax.ppermute(
+        attn_section[:, attn_columns:].reshape(-1, width), ("seq", "fsdp"), turned
+    ).astype(wide)
+    head_part = jnp.concatenate(
+        [
+            grad_decay_up.reshape(rank, shards, -1).transpose(1, 0, 2).reshape(shards, -1),
+            grad_decay_bias.reshape(shards, -1),
+        ],
+        axis=1,
+    )
+    mine = jnp.arange(parts)[:, None, None] == lax.axis_index("fsdp")
+    head_part = jnp.where(mine, head_part[None], 0.0).reshape(devices, -1)
     own_bias_size = HK // shards
-    own_up = head_part[: rank * own_bias_size].reshape(rank, own_bias_size)
-    own_bias = head_part[rank * own_bias_size :]
     summed = jnp.concatenate(
         [
             grad_attn_gain.reshape(devices, -1),
             grad_ffn_gain.reshape(devices, -1),
             grad_head_gain.reshape(devices, -1),
             grad_decay_down.reshape(devices, -1),
+            head_part,
         ],
         axis=1,
     )
-    summed = lax.psum_scatter(summed, "seq", scatter_dimension=0, tiled=True)
-    summed = lax.psum_scatter(summed, "fsdp", scatter_dimension=0, tiled=True)[0]
+    summed = jnp.sum(lax.all_to_all(summed, ("seq", "fsdp"), 0, 0), axis=0)
     each = width // devices
     each_head = HV // devices
     own_attn_gain = summed[:each]
     own_ffn_gain = summed[each : 2 * each]
     own_head_gain = summed[2 * each : 2 * each + each_head]
-    own_down = summed[2 * each + each_head :].reshape(each, rank)
+    at_up = 2 * each + each_head + each * rank
+    at_bias = at_up + rank * own_bias_size
+    own_down = summed[2 * each + each_head : at_up].reshape(each, rank)
+    own_up = summed[at_up:at_bias].reshape(rank, own_bias_size)
+    own_bias = summed[at_bias:]
     return (
         block_output[None],
         input_grad[None],

time: 668 us -> 514 us (0.77)
  waiting for transfers between devices: 388 us -> 297 us
  blocking collectives: 125 us -> 51.6 us
  local copies, waits for them, and re-layouts: 44.6 us -> 54.8 us
  matrix products: 48.6 us -> 41.2 us
  starting transfers between devices: 12.5 us -> 19.8 us
    unnamed x3 -> x0, blocking collectives: 67.8 us -> none
    unnamed x18 -> x11, waiting for transfers between devices: 49.8 us -> 0.18 us
    all_gather x4 -> x3, waiting for transfers between devices: 89.4 us -> 51.3 us  [gather_rows(): return lax.all_gather(rows, 'fsdp', axis=0, tiled=True)]
    reduce_scatter x3 -> x2, waiting for transfers between devices: 111 us -> 74 us  [summed_rows(): lax.psum_scatter(grads.astype(low), 'seq', scatter_dimension=0, tiled=True)]
    all_to_all x2 -> x3, waiting for transfers between devices: 0.01 us -> 32.9 us  [exchange(): return lax.all_to_all(pieces, 'fsdp', 0, 0)]
    all_gather x3 -> x1, waiting for transfers between devices: 72.7 us -> 42.1 us  [on_device(): got = lax.all_gather(exchange(jnp.concatenate(cuts, axis=2)), 'seq')]
    reduce_scatter x4 -> x3, waiting for transfers between devices: 41.6 us -> 70.4 us  [scatter_rows(): lax.psum_scatter(rows.astype(low), 'fsdp', scatter_dimension=0, tiled=True)]
    all_to_all x2 -> x3, starting transfers between devices: 9.2 us -> 15.7 us  [exchange(): return lax.all_to_all(pieces, 'fsdp', 0, 0)]
  transfers between devices with their start and end apart: 21 -> 16, of which waited for: 15 -> 13; matrix products, arithmetic and copies ran while one was open for 11% -> 15% of each run, Pallas kernels for 0% -> 0%
where the time goes in v2:
time: 514 us; the launch traced here: 510 us
  waiting for transfers between devices  297 us (58%)
  local copies, waits for them, and re-layouts  54.8 us (11%)
  blocking collectives  51.6 us (10%)
  matrix products  41.2 us (8%)
  other arithmetic  30.1 us (6%)
  starting transfers between devices  19.8 us (4%)
  between operations  15.2 us (3%)
    reduce_scatter x2, waiting for transfers between devices, summed_rows(): lax.psum_scatter(grads.astype(low), 'seq', scatter_dimension=0, tiled=True)  74 us
    reduce_scatter x3, waiting for transfers between devices, scatter_rows(): lax.psum_scatter(rows.astype(low), 'fsdp', scatter_dimension=0, tiled=True)  70.4 us
    all_gather x3, waiting for transfers between devices, gather_rows(): return lax.all_gather(rows, 'fsdp', axis=0, tiled=True)  51.3 us
    all_to_all x1, blocking collectives, exchange(): return lax.all_to_all(pieces, 'fsdp', 0, 0)  42.8 us
    all_gather x1, waiting for transfers between devices, on_device(): got = lax.all_gather(exchange(jnp.concatenate(cuts, axis=2)), 'seq')  42.1 us
    all_to_all x3, waiting for transfers between devices, exchange(): return lax.all_to_all(pieces, 'fsdp', 0, 0)  32.9 us
    all_gather x1, waiting for transfers between devices, on_device(): states = lax.all_gather(local_state.astype(low), 'seq')  16.6 us
    unnamed x153, local copies, waits for them, and re-layouts  16.1 us
  transfers between devices with their start and end apart: 16, of which 13 were waited for; matrix products, arithmetic and copies ran while one was open for 15% of the time, Pallas kernels for 0%

profile of v2, /device:TPU:0, one launch (start us, length us, event | category | flops | bytes accessed | tf_op | source)
XLA Modules:
  0.0 509.9 jit_solution(16468545646592086192)
XLA Ops:
  8.3 2.1 concatenate.30
  12.5 6.3 %all-to-all-start = ((bf16[4,2,2336]{2,1,0:T(2,128)(2,1)}), bf16[4,2,2336]{2,1,0:T(2,128)(2,1)S(1)}, u32[]{:S(2)}, u32[]{:S(2)}) async-start(bf16[4,2,2336]{2,1,0:T(2,128)(2,1)} %reshape.457), calls=%async_computation | async-start | bytes 77824 | tf_op jit(solution)/shard_map/all_to_all | solution.py:52
  21.1 3.4 all-to-all-done
  30.7 42.8 %all_to_all.33 = bf16[4,32,2880]{2,1,0:T(8,128)(2,1)} all-to-all(bf16[4,32,2880]{2,1,0:T(8,128)(2,1)S(1)} %copy.250), channel_id=1, replica_groups=mesh['seq'=8,'fsdp'=4] {'fsdp'}, dimensions={0} | all-to-all | bytes 1474560 | tf_op jit(solution)/shard_map/all_to_all | solution.py:52
  73.9 12.2 %all-gather.10.cloned.1.call-done = bf16[512,2048]{1,0:T(8,128)(2,1)} async-done(((bf16[128,2048]{1,0:T(8,128)(2,1)}), bf16[512,2048]{1,0:T(8,128)(2,1)}) %all-gather.10.cloned.1.call-update) | async-done | bytes 2097168 | tf_op jit(solution)/shard_map/all_gather | solution.py:56
  86.0 1.6 convolution_convert_fusion.8
  89.1 42.1 %all-gather.20.cloned.1.call-done = bf16[32,32,2880]{2,1,0:T(8,128)(2,1)} async-done(((bf16[4,32,2880]{2,1,0:T(8,128)(2,1)}), bf16[32,32,2880]{2,1,0:T(8,128)(2,1)}) %all-gather.20.cloned.1.call-update) | async-done | bytes 5898256 | tf_op jit(solution)/shard_map/all_gather | solution.py:128
  131.1 1.5 slice_bitcast_fusion.1
  132.8 2.0 copy-done.32
  134.8 2.1 fusion.70
  138.7 8.9 %all-gather.2 = f32[8,4,128]{2,1,0:T(4,128)S(1)} all-gather(f32[1,4,128]{2,1,0:T(4,128)S(1)} %bitcast.304), channel_id=3, replica_groups=mesh['seq'=8,'fsdp'=4] {'seq'}, dimensions={0}, use_global_device_ids=true | all-gather | bytes 18432 | tf_op jit(solution)/shard_map/all_gather | solution.py:174
  149.7 16.6 %all-gather.12.cloned.1.call-done = bf16[8,4,128,256]{3,2,1,0:T(8,128)(2,1)} async-done(((bf16[1,4,128,256]{3,2,1,0:T(8,128)(2,1)}), bf16[8,4,128,256]{3,2,1,0:T(8,128)(2,1)}) %all-gather.12.cloned.1.call-update) | async-done | bytes 2097168 | tf_op jit(solution)/shard_map/all_gather | solution.py:175
  166.3 2.0 multiply_reduce_fusion.1
  175.3 27.3 %reduce-scatter.8.cloned.1.call-done = bf16[128,1024]{1,0:T(8,128)(2,1)} async-done(((bf16[512,1024]{1,0:T(8,128)(2,1)}), bf16[128,1024]{1,0:T(8,128)(2,1)}) %reduce-scatter.8.cloned.1.call-update) | async-done | bytes 262160 | tf_op jit(solution)/shard_map/reduce_scatter | solution.py:60
  204.9 2.7 slice.182
  207.6 4.5 reshape.414
  212.0 2.0 copy.256
  215.4 2.1 slice_bitcast_fusion
  217.6 1.8 copy.257
  219.4 11.8 %all-gather.14.cloned.1.call-done = bf16[512,1024]{1,0:T(8,128)(2,1)} async-done(((bf16[128,1024]{1,0:T(8,128)(2,1)}), bf16[512,1024]{1,0:T(8,128)(2,1)}) %all-gather.14.cloned.1.call-update) | async-done | bytes 1048592 | tf_op jit(solution)/shard_map/all_gather | solution.py:56
  231.3 4.0 fusion.75
  235.3 1.6 fusion.2
  239.5 1.8 convolution_convert_fusion.4
  241.3 1.5 pad_maximum_fusion.1
  242.9 43.1 %reduce-scatter.10.cloned.1.call-done = bf16[128,2048]{1,0:T(8,128)(2,1)} async-done(((bf16[512,2048]{1,0:T(8,128)(2,1)}), bf16[128,2048]{1,0:T(8,128)(2,1)}) %reduce-scatter.10.cloned.1.call-update) | async-done | bytes 524304 | tf_op jit(solution)/shard_map/reduce_scatter | solution.py:60
  287.2 1.5 multiply_reduce_fusion.3
  290.0 27.3 %all-gather.16.cloned.1.call-done = bf16[512,1024]{1,0:T(8,128)(2,1)} async-done(((bf16[128,1024]{1,0:T(8,128)(2,1)}), bf16[512,1024]{1,0:T(8,128)(2,1)}) %all-gather.16.cloned.1.call-update) | async-done | bytes 1048592 | tf_op jit(solution)/shard_map/all_gather | solution.py:56
  317.3 2.8 multiply_reduce_fusion.2
  320.1 2.2 fusion.23
  324.1 3.5 convolution_convert_fusion.2
  327.5 2.6 copy.276
  330.1 3.7 convolution_convert_fusion
  333.8 2.4 pad_maximum_fusion
  341.3 9.8 %all-gather.18.cloned.1.call-done = bf16[8,4,128,256]{3,2,1,0:T(8,128)(2,1)} async-done(((bf16[1,4,128,256]{3,2,1,0:T(8,128)(2,1)}), bf16[8,4,128,256]{3,2,1,0:T(8,128)(2,1)}) %all-gather.18.cloned.1.call-update) | async-done | bytes 2097168 | tf_op jit(solution)/shard_map/all_gather | solution.py:229
  351.1 2.1 multiply_reduce_fusion
  358.1 1.5 add_convert_fusion
  360.7 2.4 convolution_convert_fusion.1
  363.1 1.6 pad_maximum_fusion.2
  364.7 4.1 copy.287
  368.8 38.3 %reduce-scatter.14.cloned.1.call-done = bf16[128,2112]{1,0:T(8,128)(2,1)} async-done(((bf16[1024,2112]{1,0:T(8,128)(2,1)}), bf16[128,2112]{1,0:T(8,128)(2,1)}) %reduce-scatter.14.cloned.1.call-update) | async-done | bytes 540688 | tf_op jit(solution)/shard_map/reduce_scatter | solution.py:64
  407.2 4.6 all-to-all-start.4
  412.1 28.0 %all-to-all-done.4 = bf16[4,32,2112]{2,1,0:T(8,128)(2,1)S(1)} async-done(((bf16[4,32,2112]{2,1,0:T(8,128)(2,1)}), bf16[4,32,2112]{2,1,0:T(8,128)(2,1)S(1)}, u32[]{:S(2)}, u32[]{:S(2)}) %all-to-all-start.4) | async-done | bytes 540704 | tf_op jit(solution)/shard_map/all_to_all | solution.py:52
  444.4 1.8 fusion.13
  448.7 2.6 all-to-all-start.2
  451.4 35.7 %reduce-scatter.16.cloned.1.call-done = bf16[128,1024]{1,0:T(8,128)(2,1)} async-done(((bf16[1024,1024]{1,0:T(8,128)(2,1)}), bf16[128,1024]{1,0:T(8,128)(2,1)}) %reduce-scatter.16.cloned.1.call-update) | async-done | bytes 262160 | tf_op jit(solution)/shard_map/reduce_scatter | solution.py:64
  487.1 1.7 slice.191
  488.7 4.7 all-to-all-start.3
  499.2 1.5 all-to-all-done.3
  (305 shorter events, 60.8 us)
Async XLA Ops:
  7.2 20.4 %copy-start = (bf16[2816,256]{1,0:T(8,128)(2,1)S(1)}, bf16[2816,256]{1,0:T(8,128)(2,1)}, u32[]{:S(2)}) copy-start(bf16[2816,256]{1,0:T(8,128)(2,1)} %param.30) | copy-start | bytes 4325380
  7.2 17.5 %copy-start.2 = (f32[1,128,1024]{2,1,0:T(8,128)S(1)}, f32[1,128,1024]{2,1,0:T(8,128)}, u32[]{:S(2)}) copy-start(f32[1,128,1024]{2,1,0:T(8,128)} %param.16) | copy-start | bytes 1572868
  12.5 12.0 %all-to-all-start = ((bf16[4,2,2336]{2,1,0:T(2,128)(2,1)}), bf16[4,2,2336]{2,1,0:T(2,128)(2,1)S(1)}, u32[]{:S(2)}, u32[]{:S(2)}) async-start(bf16[4,2,2336]{2,1,0:T(2,128)(2,1)} %reshape.457), calls=%async_computation | async-start | bytes 77824 | tf_op jit(solution)/shard_map/all_to_all | solution.py:52
  18.9 67.2 %all-gather.10.cloned.1.call-start = ((), (), s32[]{:S(2)}) async-start(), calls=%async_computation.10 | async-start | bytes 2621440 | tf_op jit(solution)/shard_map/all_gather | solution.py:56
  21.1 6.9 %copy-start.59 = (f32[128]{0:T(128)}, f32[128]{0:T(128)S(1)}, u32[]{:S(2)}) copy-start(f32[128]{0:T(128)S(1)} %fusion.56) | copy-start | bytes 1540
  25.7 105.4 %all-gather.20.cloned.1.call-start = ((), (), s32[]{:S(2)}) async-start(), calls=%async_computation.19 | async-start | bytes 6782976 | tf_op jit(solution)/shard_map/all_gather | solution.py:128
  30.6 42.9 %copy-start.68 = (bf16[128]{0:T(256)(128)(2,1)S(1)}, bf16[128]{0:T(256)(128)(2,1)}, u32[]{:S(2)}) copy-start(bf16[128]{0:T(256)(128)(2,1)} %param.24) | copy-start | bytes 772
  30.7 57.0 %copy-start.61 = (bf16[16,128]{1,0:T(8,128)(2,1)S(1)}, bf16[16,128]{1,0:T(8,128)(2,1)}, u32[]{:S(2)}) copy-start(bf16[16,128]{1,0:T(8,128)(2,1)} %param.23) | copy-start | bytes 12292
  73.5 92.9 %all-gather.12.cloned.1.call-start = ((), (), s32[]{:S(2)}) async-start(), calls=%async_computation.11 | async-start | bytes 2359296 | tf_op jit(solution)/shard_map/all_gather | solution.py:175
  73.9 14.8 %copy-start.18 = (bf16[1024,16]{1,0:T(8,128)(2,1)}, bf16[1024,16]{1,0:T(8,128)(2,1)S(1)}, u32[]{:S(2)}) copy-start(bf16[1024,16]{1,0:T(8,128)(2,1)S(1)} %reshape.406) | copy-start | bytes 98308
  87.6 45.0 %copy-start.44 = (bf16[512,16]{0,1:T(8,128)(2,1)}, bf16[512,16]{0,1:T(8,128)(2,1)S(1)}, u32[]{:S(2)}) copy-start(bf16[512,16]{0,1:T(8,128)(2,1)S(1)} %convolution_convert_fusion.8) | copy-start | bytes 49156
  89.1 79.3 %copy-start.46 = (f32[4,1,128,1]{2,1,0,3:T(1,128)}, f32[4,1,128,1]{2,1,0,3:T(1,128)S(1)}, u32[]{:S(2)}) copy-start(f32[4,1,128,1]{2,1,0,3:T(1,128)S(1)} %get-tuple-element.186) | copy-start | bytes 6148
  89.1 79.3 %copy-start.48 = (f32[4,1,128,1]{2,1,0,3:T(1,128)}, f32[4,1,128,1]{2,1,0,3:T(1,128)S(1)}, u32[]{:S(2)}) copy-start(f32[4,1,128,1]{2,1,0,3:T(1,128)S(1)} %get-tuple-element.185) | copy-start | bytes 6148
  132.8 4.2 copy-start.25
  137.0 11.6 %copy-start.3 = (bf16[512,256]{1,0:T(8,128)(2,1)}, bf16[512,256]{1,0:T(8,128)(2,1)S(1)}, u32[]{:S(2)}) copy-start(bf16[512,256]{1,0:T(8,128)(2,1)S(1)} %slice.173) | copy-start | bytes 786436
  137.0 33.3 %copy-start.8 = (bf16[512,128]{1,0:T(8,128)(2,1)}, bf16[512,128]{1,0:T(8,128)(2,1)S(1)}, u32[]{:S(2)}) copy-start(bf16[512,128]{1,0:T(8,128)(2,1)S(1)} %get-tuple-element.166) | copy-start | bytes 393220
  138.4 64.3 %reduce-scatter.8.cloned.1.call-start = ((), (), s32[]{:S(2)}) async-start(), calls=%async_computation.12 | async-start | bytes 1310720 | tf_op jit(solution)/shard_map/reduce_scatter | solution.py:60
  138.7 33.1 %copy-start.55 = (f32[256]{0:T(256)}, f32[256]{0:T(256)S(1)}, u32[]{:S(2)}) copy-start(f32[256]{0:T(256)S(1)} %reshape.439) | copy-start | bytes 3076
  148.6 17.7 %copy-start.16 = (f32[8,64,64]{2,1,0:T(8,128)}, f32[8,64,64]{2,1,0:T(8,128)S(1)}, u32[]{:S(2)}) copy-start(f32[8,64,64]{2,1,0:T(8,128)S(1)} %convolution_select_fusion.1) | copy-start | bytes 393220
  175.2 56.0 %all-gather.14.cloned.1.call-start = ((), (), s32[]{:S(2)}) async-start(), calls=%async_computation.13 | async-start | bytes 1310720 | tf_op jit(solution)/shard_map/all_gather | solution.py:56
  175.3 32.2 %copy-start.40 = (f32[1,2,4,128]{3,1,2,0:T(2,128)}, f32[1,2,4,128]{3,1,2,0:T(2,128)S(1)}, u32[]{:S(2)}) copy-start(f32[1,2,4,128]{3,1,2,0:T(2,128)S(1)} %copy.301) | copy-start | bytes 12292
  203.8 3.8 copy-start.66
  204.6 81.4 %reduce-scatter.10.cloned.1.call-start = ((), (), s32[]{:S(2)}) async-start(), calls=%async_computation.14 | async-start | bytes 2621440 | tf_op jit(solution)/shard_map/reduce_scatter | solution.py:60
  231.3 4.0 copy-start.27
  231.3 4.0 copy-start.33
  242.8 45.8 %copy-start.21 = (f32[1,128,1024]{2,1,0:T(8,128)S(1)}, f32[1,128,1024]{2,1,0:T(8,128)}, u32[]{:S(2)}) copy-start(f32[1,128,1024]{2,1,0:T(8,128)} %param.31) | copy-start | bytes 1572868
  242.8 74.5 %all-gather.16.cloned.1.call-start = ((), (), s32[]{:S(2)}) async-start(), calls=%async_computation.15 | async-start | bytes 1310720 | tf_op jit(solution)/shard_map/all_gather | solution.py:56
  290.0 30.1 %copy-start.51 = (f32[512]{0:T(512)S(1)}, f32[512]{0:T(512)}, u32[]{:S(2)}) copy-start(f32[512]{0:T(512)} %copy-done.50) | copy-start | bytes 6148
  290.0 30.1 %copy-start.53 = (f32[512]{0:T(512)S(1)}, f32[512]{0:T(512)}, u32[]{:S(2)}) copy-start(f32[512]{0:T(512)} %copy-done.52) | copy-start | bytes 6148
  290.0 30.1 %copy-start.56 = (f32[256]{0:T(256)S(1)}, f32[256]{0:T(256)}, u32[]{:S(2)}) copy-start(f32[256]{0:T(256)} %copy-done.55) | copy-start | bytes 3076
  290.0 61.1 %all-gather.18.cloned.1.call-start = ((), (), s32[]{:S(2)}) async-start(), calls=%async_computation.16 | async-start | bytes 2359296 | tf_op jit(solution)/shard_map/all_gather | solution.py:229
  323.8 83.4 %reduce-scatter.14.cloned.1.call-start = ((), (), s32[]{:S(2)}) async-start(), calls=%async_computation.18 | async-start | bytes 5013504 | tf_op jit(solution)/shard_map/reduce_scatter | solution.py:64
  336.3 110.2 %reduce-scatter.12.cloned.1.call-start = ((), (), s32[]{:S(2)}) async-start(), calls=%async_computation.17 | async-start | bytes 1310720 | tf_op jit(solution)/shard_map/reduce_scatter | solution.py:60
  339.9 13.3 %copy-start.47 = (f32[4,1,128,1]{2,1,0,3:T(1,128)S(1)}, f32[4,1,128,1]{2,1,0,3:T(1,128)}, u32[]{:S(2)}) copy-start(f32[4,1,128,1]{2,1,0,3:T(1,128)} %copy-done.46) | copy-start | bytes 6148
  359.6 127.5 %reduce-scatter.16.cloned.1.call-start = ((), (), s32[]{:S(2)}) async-start(), calls=%async_computation.20 | async-start | bytes 2359296 | tf_op jit(solution)/shard_map/reduce_scatter | solution.py:64
  368.8 43.1 %copy-start.54 = (f32[1024]{0:T(1024)S(1)}, f32[1024]{0:T(1024)}, u32[]{:S(2)}) copy-start(f32[1024]{0:T(1024)} %get-tuple-element.146) | copy-start | bytes 12292
  368.8 43.2 %copy-start.63 = (f32[256]{0:T(256)S(1)}, f32[256]{0:T(256)}, u32[]{:S(2)}) copy-start(f32[256]{0:T(256)} %get-tuple-element.144) | copy-start | bytes 3076
  407.2 32.9 %all-to-all-start.4 = ((bf16[4,32,2112]{2,1,0:T(8,128)(2,1)}), bf16[4,32,2112]{2,1,0:T(8,128)(2,1)S(1)}, u32[]{:S(2)}, u32[]{:S(2)}) async-start(bf16[4,32,2112]{2,1,0:T(8,128)(2,1)} %bitcast.265), calls=%async_computation.8 | async-start | bytes 1114112 | tf_op jit(solution)/shard_map/all_to_all | solution.py:52
  440.5 3.9 copy-start.43
  442.7 3.8 copy-start.60
  444.2 7.2 %copy-start.65 = (f32[128]{0:T(128)S(1)}, f32[128]{0:T(128)}, u32[]{:S(2)}) copy-start(f32[128]{0:T(128)} %copy-done.64) | copy-start | bytes 1540
  444.4 49.0 %copy-start.20 = (f32[128,1024]{1,0:T(8,128)S(1)}, f32[128,1024]{1,0:T(8,128)}, u32[]{:S(2)}) copy-start(f32[128,1024]{1,0:T(8,128)} %get-tuple-element.155) | copy-start | bytes 1572868
  446.5 46.9 %copy-start.29 = (bf16[128,1024]{1,0:T(8,128)(2,1)S(1)}, bf16[128,1024]{1,0:T(8,128)(2,1)}, u32[]{:S(2)}) copy-start(bf16[128,1024]{1,0:T(8,128)(2,1)} %reduce-scatter.12.cloned.1.call-done) | copy-start | bytes 786436
  448.7 40.0 %all-to-all-start.2 = ((f32[32,1,856]{2,1,0:T(1,128)}), f32[32,1,856]{2,1,0:T(1,128)S(1)}, u32[]{:S(2)}, u32[]{:S(2)}) async-start(f32[32,1,856]{2,1,0:T(1,128)} %copy.268), calls=%async_computation.5 | async-start | bytes 229376 | tf_op jit(solution)/shard_map/all_to_all | solution.py:298
  487.0 7.4 %slice-start = ((bf16[128,1024]{1,0:T(8,128)(2,1)}), bf16[128,256]{1,0:T(8,128)(2,1)S(1)}, s32[]{:S(2)}) async-start(bf16[128,1024]{1,0:T(8,128)(2,1)} %reduce-scatter.16.cloned.1.call-done), calls=%async_computation.21 | async-start | bytes 131072 | tf_op jit(solution)/shard_map/slice | solution.py:276
  488.7 14.7 %copy-start.1 = (bf16[2816,256]{1,0:T(8,128)(2,1)S(1)}, bf16[2816,256]{1,0:T(8,128)(2,1)}, u32[]{:S(2)}) copy-start(bf16[2816,256]{1,0:T(8,128)(2,1)} %param.30) | copy-start | bytes 4325380
  488.7 12.0 %all-to-all-start.3 = ((bf16[4,32,768]{2,1,0:T(8,128)(2,1)}), bf16[4,32,768]{2,1,0:T(8,128)(2,1)S(1)}, u32[]{:S(2)}, u32[]{:S(2)}) async-start(bf16[4,32,768]{2,1,0:T(8,128)(2,1)} %bitcast.55), calls=%async_computation.6 | async-start | bytes 393216 | tf_op jit(solution)/shard_map/all_to_all | solution.py:52
  494.6 4.0 collective-permute-start
  (41 other events, 77.5 us)
Sparse Core Ops, SparseCore 0:
  25.8 60.1 all-gather.9
  87.9 43.1 all-gather.19
  138.5 27.7 all-gather.11
  175.3 27.2 reduce-scatter.7
  204.7 26.4 all-gather.13
  243.0 42.9 reduce-scatter.9
  290.1 27.1 all-gather.15
  323.9 27.1 all-gather.17
  354.6 52.5 reduce-scatter.13
  409.3 34.4 reduce-scatter.11
  447.1 39.9 reduce-scatter.15
